TPU v7x, 32 devices: a whole 2x2x4 slice. The times are simulated.
32 devices in a mesh: rows: 4 (over z), cols: 8 (over y, x, core).
Axes of the slice: x: 2, y: 2, z: 4, core: 2. Of those that a mesh axis runs over, the one named last changes fastest.
Arguments:
- imagery: bfloat16 [64, 128, 192], P('rows', 'cols'), may hold values from -6 to 6
- cotangent: bfloat16 [64, 128, 192], P('rows', 'cols'), may hold values from -6 to 6
- norm_gain: float32 [2, 192], replicated, may hold values from 0.5 to 1.5
- norm_bias: float32 [2, 192], replicated, may hold values from -3 to 3
- qkv_weight: bfloat16 [2, 192, 576], replicated, may hold values from -0.4375 to 0.4375
- qkv_bias: float32 [2, 576], replicated, may hold values from -3 to 3
- rel_table: float32 [2, 6, 225], replicated, may hold values from -4 to 330
- proj_weight: bfloat16 [2, 192, 192], replicated, may hold values from -0.4375 to 0.4375
- proj_bias: float32 [2, 192], replicated, may hold values from -3 to 3
- mlp_gain: float32 [2, 192], replicated, may hold values from 0.5 to 1.5
- mlp_bias: float32 [2, 192], replicated, may hold values from -3 to 3
- up_weight: bfloat16 [2, 192, 768], replicated, may hold values from -0.4375 to 0.4375
- up_bias: float32 [2, 768], replicated, may hold values from -3 to 3
- down_weight: bfloat16 [2, 768, 192], replicated, may hold values from -0.21875 to 0.21875
- down_bias: float32 [2, 192], replicated, may hold values from -3 to 3
Outputs:
- output: bfloat16 [64, 128, 192], P('rows', 'cols')
- imagery_grad: bfloat16 [64, 128, 192], P('rows', 'cols')
- norm_gain_grad: float32 [2, 192], replicated
- norm_bias_grad: float32 [2, 192], replicated
- qkv_weight_grad: float32 [2, 192, 576], replicated
- qkv_bias_grad: float32 [2, 576], replicated
- rel_table_grad: float32 [2, 6, 225], replicated
- proj_weight_grad: float32 [2, 192, 192], replicated
- proj_bias_grad: float32 [2, 192], replicated
- mlp_gain_grad: float32 [2, 192], replicated
- mlp_bias_grad: float32 [2, 192], replicated
- up_weight_grad: float32 [2, 192, 768], replicated
- up_bias_grad: float32 [2, 768], replicated
- down_weight_grad: float32 [2, 768, 192], replicated
- down_bias_grad: float32 [2, 192], replicated
All inputs are finite; a program needn't handle non-finite values.
Results may differ from a plain program's by a relative error of at most 0.02.
Values may be sent and summed in bfloat16 or wider, within the bound.
A program may use at most 128 MiB of HBM per device.

v0:
```python
import functools

import jax
import jax.numpy as jnp
from jax import lax
from jax.experimental import pallas as pl
from jax.experimental.pallas import tpu as pltpu
from jax.sharding import PartitionSpec as P

WIN = 8
EPSILON = 1e-05
F32 = jnp.float32
BF16 = jnp.bfloat16
MESH = pl.DeviceIdType.MESH


def mm(a, b):
    return jnp.dot(a, b, preferred_element_type=F32)


def mm_nt(a, b):
    return lax.dot_general(a, b, (((1,), (1,)), ((), ())), preferred_element_type=F32)


def mm_tn(a, b):
    return lax.dot_general(a, b, (((0,), (0,)), ((), ())), preferred_element_type=F32)


def split3(x):
    hi = x.astype(BF16)
    rest = x - hi.astype(F32)
    mid = rest.astype(BF16)
    return hi, mid, (rest - mid.astype(F32)).astype(BF16)


def load_windows(ref, height, breadth):
    parts = []
    for r in range(0, height, WIN):
        for c in range(0, breadth, WIN):
            piece = ref[r : r + WIN, c : c + WIN, :].astype(F32)
            parts.append(piece.reshape(WIN * WIN, piece.shape[-1]))
    return jnp.concatenate(parts, axis=0)


def store_windows(ref, values, height, breadth):
    at = 0
    for r in range(0, height, WIN):
        for c in range(0, breadth, WIN):
            piece = values[at : at + WIN * WIN].reshape(WIN, WIN, values.shape[-1])
            ref[r : r + WIN, c : c + WIN, :] = piece.astype(ref.dtype)
            at += WIN * WIN


def norm_parts(x):
    center = x - jnp.mean(x, axis=-1, keepdims=True)
    spread = jnp.mean(center * center, axis=-1, keepdims=True)
    inv = lax.rsqrt(spread + EPSILON)
    return center * inv, inv


def norm_back(unit, inv, gain, grad):
    scaled = grad * gain
    m1 = jnp.mean(scaled, axis=-1, keepdims=True)
    m2 = jnp.mean(scaled * unit, axis=-1, keepdims=True)
    return inv * (scaled - m1 - unit * m2)


def rnd(x):
    return x.astype(BF16).astype(F32)


def head_rows(rows, heads, size):
    lane = lax.broadcasted_iota(jnp.int32, (heads * rows, heads * size), 1)
    row = lax.broadcasted_iota(jnp.int32, (heads * rows, heads * size), 0)
    return (lane // size) == (row // rows)


def spread_heads(x, mask, heads):
    tiled = jnp.concatenate([x] * heads, axis=0)
    return jnp.where(mask, tiled, jnp.zeros_like(tiled))


def fold_heads(x, mask, heads, rows):
    kept = jnp.where(mask, x, 0.0)
    total = kept[:rows]
    for h in range(1, heads):
        total = total + kept[h * rows : (h + 1) * rows]
    return total


def cell_code(n, dim, shape):
    index = lax.broadcasted_iota(jnp.int32, shape, dim)
    return (index // WIN) * (2 * WIN - 1) + index % WIN


def position_stack(rel, heads):
    cells = WIN * WIN
    span = 2 * WIN - 1
    middle = (span * span - 1) // 2
    width = 256
    lanes = lax.broadcasted_iota(jnp.int32, (cells, 128), 1)
    pick = (lanes == cell_code(cells, 0, (cells, 128))).astype(BF16)
    outs = []
    for h in range(heads):
        row = jnp.concatenate([rel[h : h + 1], jnp.zeros((1, width - span * span), F32)], axis=1)
        row = jnp.broadcast_to(row, (WIN, width))
        rolled = [
            pltpu.roll(row, (span * y - middle) % width, 1, stride=1, stride_axis=0)[:, :128]
            for y in range(WIN)
        ]
        parts = split3(jnp.concatenate(rolled, axis=0))
        outs.append(mm_nt(pick, parts[0]) + mm_nt(pick, parts[1]) + mm_nt(pick, parts[2]))
    return jnp.concatenate(outs, axis=0)


def position_grad(dstack, heads):
    cells = WIN * WIN
    span = 2 * WIN - 1
    middle = (span * span - 1) // 2
    width = 256
    lanes = lax.broadcasted_iota(jnp.int32, (cells, width), 1)
    pick = (lanes == middle - cell_code(cells, 0, (cells, width))).astype(BF16)
    rows = []
    for h in range(heads):
        hi, mid, _ = split3(dstack[h * cells : (h + 1) * cells])
        flipped = mm_tn(hi, pick) + mm_tn(mid, pick)
        total = None
        for y in range(WIN):
            part = pltpu.roll(
                flipped[y * WIN : (y + 1) * WIN], span * y, 1, stride=1, stride_axis=0
            )
            total = part if total is None else total + part
        rows.append(jnp.sum(total, axis=0, keepdims=True))
    rows.append(jnp.zeros((16 - heads, width), F32))
    stacked = jnp.concatenate(rows, axis=0)
    back = (
        lax.broadcasted_iota(jnp.int32, (width, width), 0)
        + lax.broadcasted_iota(jnp.int32, (width, width), 1)
        == span * span - 1
    ).astype(BF16)
    hi, mid, _ = split3(stacked)
    return mm(hi, back) + mm(mid, back)


def zone_masks(start_ref, height, breadth, total_rows, total_cols, heads):
    cells = WIN * WIN
    masks = []
    for r in range(0, height, WIN):
        for c in range(0, breadth, WIN):

            def zone(dim):
                index = lax.broadcasted_iota(jnp.int32, (heads * cells, cells), dim) % cells
                row = start_ref[0] + r + index // WIN
                col = start_ref[1] + c + index % WIN
                zr = (row >= total_rows - WIN).astype(jnp.int32) + (
                    row >= total_rows - WIN // 2
                ).astype(jnp.int32)
                zc = (col >= total_cols - WIN).astype(jnp.int32) + (
                    col >= total_cols - WIN // 2
                ).astype(jnp.int32)
                return zr * 3 + zc

            masks.append(zone(0) == zone(1))
    return masks


def attend(q_stack, k, position, mask, scale):
    scores = mm_nt(q_stack, k) * scale + position
    if mask is not None:
        scores = jnp.where(mask, scores, -1e30)
    powers = jnp.exp(scores - jnp.max(scores, axis=-1, keepdims=True))
    return powers / jnp.sum(powers, axis=-1, keepdims=True)


def forward(x, w, position, masks, heads):
    cells = WIN * WIN
    channels = x.shape[1]
    size = channels // heads
    unit, _ = norm_parts(x)
    normed = (unit * w["ng"][...] + w["nb"][...]).astype(BF16)
    packed = (mm(normed, w["wqkv"][0]) + w["bqkv"][...]).astype(BF16)
    hmask = head_rows(cells, heads, size)
    mixed = []
    for n in range(x.shape[0] // cells):
        at = slice(n * cells, (n + 1) * cells)
        q = packed[at, :channels]
        k = packed[at, channels : 2 * channels]
        v = packed[at, 2 * channels :]
        probs = attend(
            spread_heads(q, hmask, heads), k, position, None if masks is None else masks[n],
            size ** (-0.5),
        )
        mixed.append(fold_heads(mm(probs.astype(BF16), v), hmask, heads, cells).astype(BF16))
    mixed = jnp.concatenate(mixed, axis=0)
    mid = (x + mm(mixed, w["wproj"][0]) + w["bproj"][...]).astype(BF16)
    mid32 = mid.astype(F32)
    unit2, _ = norm_parts(mid32)
    normed2 = (unit2 * w["mg"][...] + w["mb"][...]).astype(BF16)
    pre = mm(normed2, w["wup"][0]) + w["bup"][...]
    half = 0.5 * (1.0 + lax.erf(pre * (2.0**-0.5)))
    hidden = (pre * half).astype(BF16)
    out = (mid32 + mm(hidden, w["wdown"][0]) + w["bdown"][...]).astype(BF16)
    return out, (packed, mixed, mid, pre)


def backward(x, g, saved, w, position, masks, heads, grads_ref, light_ref):
    packed, mixed, mid, pre = saved
    cells = WIN * WIN
    channels = x.shape[1]
    size = channels // heads
    scale = size ** (-0.5)
    light_ref[...] = jnp.zeros_like(light_ref)
    g16 = g.astype(BF16)
    half = 0.5 * (1.0 + lax.erf(pre * (2.0**-0.5)))
    slope = half + pre * jnp.exp(-0.5 * pre * pre) * 0.3989422804014327
    hidden = (pre * half).astype(BF16)
    grads_ref[2 * channels : 3 * channels, :] = mm_tn(g16, hidden).astype(BF16)
    light_ref[3:4, :channels] = jnp.sum(g, axis=0, keepdims=True)
    dpre = rnd(mm_nt(g16, w["wdown"][0])) * slope
    light_ref[0:1, : dpre.shape[1]] = jnp.sum(dpre, axis=0, keepdims=True)
    dpre16 = dpre.astype(BF16)
    mid32 = mid.astype(F32)
    unit2, inv2 = norm_parts(mid32)
    normed2 = (unit2 * w["mg"][...] + w["mb"][...]).astype(BF16)
    grads_ref[channels : 2 * channels, :] = mm_tn(normed2, dpre16).astype(BF16)
    dn2 = rnd(mm_nt(dpre16, w["wup"][0]))
    light_ref[2:3, 2 * channels : 3 * channels] = jnp.sum(dn2 * unit2, axis=0, keepdims=True)
    light_ref[2:3, 3 * channels : 4 * channels] = jnp.sum(dn2, axis=0, keepdims=True)
    dmid = rnd(rnd(norm_back(unit2, inv2, w["mg"][...], dn2)) + g)
    dmid16 = dmid.astype(BF16)
    light_ref[1:2, 3 * channels : 4 * channels] = jnp.sum(dmid, axis=0, keepdims=True)
    grads_ref[0:channels, 3 * channels : 4 * channels] = mm_tn(mixed, dmid16).astype(BF16)
    dmixed = mm_nt(dmid16, w["wproj"][0]).astype(BF16)
    hmask = head_rows(cells, heads, size)
    dpacked = []
    dposition = None
    for n in range(x.shape[0] // cells):
        at = slice(n * cells, (n + 1) * cells)
        q_stack = spread_heads(packed[at, :channels], hmask, heads)
        k = packed[at, channels : 2 * channels]
        v = packed[at, 2 * channels :]
        probs = attend(q_stack, k, position, None if masks is None else masks[n], scale)
        d_stack = spread_heads(dmixed[at], hmask, heads)
        dprobs = rnd(mm_nt(d_stack, v))
        dv = mm_tn(probs.astype(BF16), d_stack)
        ds = probs * (dprobs - jnp.sum(probs * dprobs, axis=-1, keepdims=True))
        dposition = ds if dposition is None else dposition + ds
        ds16 = (ds * scale).astype(BF16)
        dq = fold_heads(mm(ds16, k), hmask, heads, cells)
        dk = mm_tn(ds16, q_stack)
        dpacked.append(jnp.concatenate([dq, dk, dv], axis=1).astype(BF16))
    light_ref[4 : 4 + 12, 0:256] = position_grad(dposition, heads)[:12]
    dpacked = jnp.concatenate(dpacked, axis=0)
    light_ref[1:2, : 3 * channels] = jnp.sum(dpacked.astype(F32), axis=0, keepdims=True)
    unit, inv = norm_parts(x)
    normed = (unit * w["ng"][...] + w["nb"][...]).astype(BF16)
    grads_ref[0:channels, : 3 * channels] = mm_tn(normed, dpacked).astype(BF16)
    dn = rnd(mm_nt(dpacked, w["wqkv"][0]))
    light_ref[2:3, 0:channels] = jnp.sum(dn * unit, axis=0, keepdims=True)
    light_ref[2:3, channels : 2 * channels] = jnp.sum(dn, axis=0, keepdims=True)
    dx = rnd(norm_back(unit, inv, w["ng"][...], dn)) + dmid
    grads_ref[3 * channels : 3 * channels + 16, :] = light_ref[...].astype(BF16)
    rest = grads_ref.shape[0] - 3 * channels - 16
    if rest:
        grads_ref[3 * channels + 16 :, :] = jnp.zeros((rest, grads_ref.shape[1]), BF16)
    return dx


KEYS = ("ng", "nb", "wqkv", "bqkv", "rel", "wproj", "bproj", "mg", "mb", "wup", "bup", "wdown", "bdown")
MATRICES = ("wqkv", "rel", "wproj", "wup", "wdown")


def weight_view(refs, block):
    view = {}
    for key, ref in zip(KEYS, refs):
        view[key] = ref if key in MATRICES else ref.at[block : block + 1, :]
    return view


def weight_specs(params, block):
    specs = []
    for key, member in zip(KEYS, params):
        if key in MATRICES:
            specs.append(pl.BlockSpec((1,) + member.shape[1:], lambda i: (block, 0, 0)))
        else:
            specs.append(pl.BlockSpec(member.shape, lambda i: (0, 0)))
    return specs


def whole(shape):
    return pl.BlockSpec(shape, lambda i: (0,) * len(shape))


def shape_of(shape, dtype):
    return jax.ShapeDtypeStruct(shape, dtype)


def first_forward(imagery, params):
    height, breadth, channels = imagery.shape
    heads = params[4].shape[1]
    tokens = height * breadth
    mlp = params[9].shape[2]

    def body(x_ref, *refs):
        w = weight_view(refs[: len(KEYS)], 0)
        out_ref, packed_ref, mixed_ref, mid_ref, pre_ref, pos_ref = refs[len(KEYS) :]
        x = load_windows(x_ref, height, breadth)
        position = position_stack(w["rel"][0], heads)
        pos_ref[...] = position
        out, saved = forward(x, w, position, None, heads)
        store_windows(out_ref, out.astype(F32), height, breadth)
        for ref, value in zip((packed_ref, mixed_ref, mid_ref, pre_ref), saved):
            ref[...] = value

    outs = [
        shape_of(imagery.shape, BF16),
        shape_of((tokens, 3 * channels), BF16),
        shape_of((tokens, channels), BF16),
        shape_of((tokens, channels), BF16),
        shape_of((tokens, mlp), F32),
        shape_of((heads * WIN * WIN, WIN * WIN), F32),
    ]
    return pl.pallas_call(
        body,
        name="fwd0",
        grid=(1,),
        out_shape=outs,
        in_specs=[whole(imagery.shape)] + weight_specs(params, 0),
        out_specs=[whole(o.shape) for o in outs],
    )(imagery, *params)


def second_both(moved, grad, start, params, total_rows, total_cols, grad_rows):
    height, breadth, channels = moved.shape
    heads = params[4].shape[1]
    width = params[9].shape[2]

    def body(start_ref, x_ref, g_ref, *refs):
        w = weight_view(refs[: len(KEYS)], 1)
        out_ref, dx_ref, grads_ref, light_ref = refs[len(KEYS) :]
        x = load_windows(x_ref, height, breadth)
        position = position_stack(w["rel"][0], heads)
        masks = zone_masks(start_ref, height, breadth, total_rows, total_cols, heads)
        out, saved = forward(x, w, position, masks, heads)
        store_windows(out_ref, out.astype(F32), height, breadth)
        g = load_windows(g_ref, height, breadth)
        dx = backward(x, g, saved, w, position, masks, heads, grads_ref, light_ref)
        store_windows(dx_ref, dx, height, breadth)

    outs = [
        shape_of(moved.shape, BF16),
        shape_of(moved.shape, BF16),
        shape_of((grad_rows, width), BF16),
    ]
    return pl.pallas_call(
        body,
        name="both1",
        grid=(1,),
        out_shape=outs,
        in_specs=[pl.BlockSpec(memory_space=pltpu.SMEM), whole(moved.shape), whole(moved.shape)]
        + weight_specs(params, 1),
        out_specs=[whole(o.shape) for o in outs],
        scratch_shapes=[pltpu.VMEM((16, width), F32)],
    )(start, moved, grad, *params)


def first_backward(imagery, grad, saved, params, grad_rows):
    height, breadth, channels = imagery.shape
    heads = params[4].shape[1]
    width = params[9].shape[2]

    def body(x_ref, g_ref, packed_ref, mixed_ref, mid_ref, pre_ref, pos_ref, *refs):
        w = weight_view(refs[: len(KEYS)], 0)
        dx_ref, grads_ref, light_ref = refs[len(KEYS) :]
        x = load_windows(x_ref, height, breadth)
        g = load_windows(g_ref, height, breadth)
        values = (packed_ref[...], mixed_ref[...], mid_ref[...], pre_ref[...])
        dx = backward(x, g, values, w, pos_ref[...], None, heads, grads_ref, light_ref)
        store_windows(dx_ref, dx, height, breadth)

    outs = [shape_of(imagery.shape, BF16), shape_of((grad_rows, width), BF16)]
    return pl.pallas_call(
        body,
        name="bwd0",
        grid=(1,),
        out_shape=outs,
        in_specs=[whole(imagery.shape), whole(grad.shape)]
        + [whole(s.shape) for s in saved]
        + weight_specs(params, 0),
        out_specs=[whole(o.shape) for o in outs],
        scratch_shapes=[pltpu.VMEM((16, width), F32)],
    )(imagery, grad, *saved, *params)


def sum_all(grads_one, grads_two, nz, nq):
    block_rows, width = grads_one.shape
    rows = 2 * block_rows
    half = width // 2
    part = rows // nq
    piece = part // nz

    def body(one_ref, two_ref, out_ref, buf0, acc, buf1, acc1, buf2, send, recv):
        z = lax.axis_index("rows")
        col = lax.axis_index("cols")
        core = lax.rem(col, 2)
        q = col // 2
        mine = pl.multiple_of(core * half, 128)
        other = pl.multiple_of((1 - core) * half, 128)
        partner = (z, q * 2 + (1 - core))
        across = [(z, lax.rem(q + d, nq) * 2 + core) for d in range(1, nq)]
        along = [(lax.rem(z + d, nz), col) for d in range(1, nz)]
        barrier = pltpu.get_barrier_semaphore()
        for peer in [partner] + across + along:
            pl.semaphore_signal(barrier, inc=1, device_id=peer, device_id_type=MESH)
        pl.semaphore_wait(barrier, nq + nz - 1)

        def copy(src, dst, index, peer):
            c = pltpu.make_async_remote_copy(
                src_ref=src,
                dst_ref=dst,
                send_sem=send.at[index],
                recv_sem=recv.at[index],
                device_id=peer,
                device_id_type=MESH,
            )
            c.start()
            return c

        sem = 0
        copies = []
        for b, ref in enumerate((one_ref, two_ref)):
            copies.append(
                copy(ref.at[:, pl.ds(other, half)], buf0.at[pl.ds(b * block_rows, block_rows), :], sem, partner)
            )
            sem += 1
        for b, ref in enumerate((one_ref, two_ref)):
            copies[b].wait()
            at = pl.ds(b * block_rows, block_rows)
            acc[at, :] = (ref[:, pl.ds(mine, half)].astype(F32) + buf0[at, :].astype(F32)).astype(BF16)
        copies = []
        for d in range(1, nq):
            to = pl.multiple_of(lax.rem(q + d, nq) * part, 16)
            copies.append(copy(acc.at[pl.ds(to, part), :], buf1.at[d - 1], sem, across[d - 1]))
            sem += 1
        total = acc[pl.ds(pl.multiple_of(q * part, 16), part), :].astype(F32)
        for d in range(1, nq):
            copies[d - 1].wait()
            total = total + buf1[d - 1].astype(F32)
        acc1[...] = total.astype(BF16)
        copies = []
        for d in range(1, nz):
            to = pl.multiple_of(lax.rem(z + d, nz) * piece, 16)
            copies.append(copy(acc1.at[pl.ds(to, piece), :], buf2.at[d - 1], sem, along[d - 1]))
            sem += 1
        total = acc1[pl.ds(pl.multiple_of(z * piece, 16), piece), :].astype(F32)
        for d in range(1, nz):
            copies[d - 1].wait()
            total = total + buf2[d - 1].astype(F32)
        lanes = pl.ds(mine, half)
        own = pl.ds(pl.multiple_of(q * part + z * piece, 16), piece)
        out_ref[own, lanes] = total.astype(BF16)
        copies = []
        for d in range(1, nz):
            copies.append(copy(out_ref.at[own, lanes], out_ref.at[own, lanes], sem, along[d - 1]))
            sem += 1
        for c in copies:
            c.wait()
        copies = []
        own = pl.ds(pl.multiple_of(q * part, 16), part)
        for d in range(1, nq):
            copies.append(copy(out_ref.at[own, lanes], out_ref.at[own, lanes], sem, across[d - 1]))
            sem += 1
        for c in copies:
            c.wait()
        copy(out_ref.at[:, lanes], out_ref.at[:, lanes], sem, partner).wait()

    sems = 2 + 2 * (nq - 1) + 2 * (nz - 1) + 1
    vmem = pl.BlockSpec(memory_space=pltpu.VMEM)
    return pl.pallas_call(
        body,
        name="sum_all",
        out_shape=shape_of((rows, width), BF16),
        in_specs=[vmem, vmem],
        out_specs=vmem,
        scratch_shapes=[
            pltpu.VMEM((rows, half), BF16),
            pltpu.VMEM((rows, half), BF16),
            pltpu.VMEM((max(nq - 1, 1), part, half), BF16),
            pltpu.VMEM((part, half), BF16),
            pltpu.VMEM((max(nz - 1, 1), piece, half), BF16),
            pltpu.SemaphoreType.DMA((sems,)),
            pltpu.SemaphoreType.DMA((sems,)),
        ],
        compiler_params=pltpu.CompilerParams(collective_id=0, has_side_effects=True),
    )(grads_one, grads_two)


def unpack(summed, params, factor):
    channels = params[0].shape[1]
    heads, offsets = params[4].shape[1:]
    block_rows = summed.shape[0] // 2

    def body(s_ref, *outs):
        o = dict(zip(KEYS, outs))
        for b in range(2):
            at = b * block_rows

            def rows(low, count):
                return s_ref[at + low : at + low + count, :].astype(F32) * factor

            top = rows(0, channels)
            o["wqkv"][b] = top[:, : 3 * channels]
            o["wproj"][b] = top[:, 3 * channels :]
            o["wup"][b] = rows(channels, channels)
            o["wdown"][b] = rows(2 * channels, channels).T
            light = rows(3 * channels, 16)
            o["bup"][b : b + 1, :] = light[0:1, :]
            o["bqkv"][b : b + 1, :] = light[1:2, : 3 * channels]
            o["bproj"][b : b + 1, :] = light[1:2, 3 * channels :]
            for place, key in enumerate(("ng", "nb", "mg", "mb")):
                o[key][b : b + 1, :] = light[2:3, place * channels : (place + 1) * channels]
            o["bdown"][b : b + 1, :] = light[3:4, :channels]
            o["rel"][b] = light[4 : 4 + heads, :offsets]

    outs = [shape_of(member.shape, F32) for member in params]
    return pl.pallas_call(
        body,
        name="unpack",
        grid=(1,),
        out_shape=outs,
        in_specs=[whole(summed.shape)],
        out_specs=[whole(o.shape) for o in outs],
    )(summed)


def from_behind(value, axis, steps):
    count = lax.axis_size(axis)
    pairs = [(source, (source + steps) % count) for source in range(count)]
    return lax.ppermute(value, axis, pairs)


def along_axis(values, axis, name, direction):
    half = WIN // 2
    size = values.shape[axis]
    if direction < 0:
        outgoing = lax.slice_in_dim(values, 0, half, axis=axis)
        kept = lax.slice_in_dim(values, half, size, axis=axis)
    else:
        outgoing = lax.slice_in_dim(values, size - half, size, axis=axis)
        kept = lax.slice_in_dim(values, 0, size - half, axis=axis)
    arrived = from_behind(outgoing, name, direction)
    return jnp.concatenate([kept, arrived] if direction < 0 else [arrived, kept], axis=axis)


def advance(values):
    return along_axis(along_axis(values, 0, "rows", -1), 1, "cols", -1)


def retreat(values):
    return along_axis(along_axis(values, 0, "rows", 1), 1, "cols", 1)


def per_device(imagery, cotangent, *params):
    height, breadth, channels = imagery.shape
    nz = lax.axis_size("rows")
    nc = lax.axis_size("cols")
    total_rows = height * nz
    total_cols = breadth * nc
    start = jnp.stack(
        [lax.axis_index("rows") * height, lax.axis_index("cols") * breadth]
    ).astype(jnp.int32)
    unit = nz * (nc // 2) * 8
    grad_rows = -(-(3 * channels + 16) // unit) * unit
    level_one, *saved = first_forward(imagery, params)
    level_two, back_two, grads_two = second_both(
        advance(level_one), advance(cotangent), start, params, total_rows, total_cols, grad_rows
    )
    output = retreat(level_two)
    back_one, grads_one = first_backward(imagery, retreat(back_two), saved, params, grad_rows)
    summed = sum_all(grads_one, grads_two, nz, nc // 2)
    merged = unpack(summed, params, float(total_rows * total_cols) ** (-0.5))
    return (output, back_one) + tuple(merged)


def solution(mesh):
    tile = P("rows", "cols", None)
    return jax.shard_map(
        per_device,
        mesh=mesh,
        in_specs=(tile, tile) + (P(),) * 13,
        out_specs=(tile, tile) + (P(),) * 13,
        check_vma=False,
    )
```

profile of v0, /device:TPU:0, one launch (start us, length us, event | category | flops | bytes accessed | tf_op | source)
XLA Modules:
  0.0 103.0 jit_solution(13885868258464317883)
XLA Ops:
  0.6 0.8 slice.53
  1.4 5.1 %collective-permute-start.2 = (bf16[4,16,192]{2,1,0:T(8,128)(2,1)S(1)}, bf16[4,16,192]{2,1,0:T(8,128)(2,1)S(1)}, u32[]{:S(2)}, u32[]{:S(2)}) collective-permute-start(bf16[4,16,192]{2,1,0:T(8,128)(2,1)S(1)} %slice.53), channel_id=1, source_target_pairs={{0,24},{8,0},{16,8},{24,16},{1,25},{9,1},{17,9},{25,17},{2,26},{10... | collective-permute-start | bytes 73736 | tf_op jit(solution)/shard_map/ppermute | solution.py:539
  6.5 1.3 %copy.30.refs_4_ = f32[2,6,225]{2,1,0:T(8,128)} copy(f32[2,6,225]{2,0,1:T(2,128)} %param.21) | data formatting | bytes 21600 | tf_op args[6]
  7.8 2.3 %copy.31.refs_11_ = bf16[2,768,192]{2,1,0:T(8,128)(2,1)} copy(bf16[2,768,192]{1,2,0:T(8,128)(2,1)} %param.28) | data formatting | bytes 1179648 | tf_op args[13]
  10.0 4.4 %fwd0.1 = (bf16[16,16,192]{2,1,0:T(8,128)(2,1)}, bf16[256,576]{1,0:T(8,128)(2,1)}, bf16[256,192]{1,0:T(8,128)(2,1)}, bf16[256,192]{1,0:T(8,128)(2,1)}, f32[256,768]{1,0:T(8,128)}, /*index=5*/f32[384,64]{1,0:T(8,128)}) custom-call(bf16[16,16,192]{2,1,0:T(8,128)(2,1)} %x_ref.3, f32[2,192]{1,0:T(2,128)} %refs_0_.5, f32[2,192]{1,0:T(2,128)} %refs_1_.5, ...), custom_call_target="tpu_custom_call" | custom-call | tf_op jit(solution)/shard_map/fwd0/pallas_call | solution.py:323
  14.5 0.8 slice.49
  15.2 0.5 collective-permute-start
  15.7 0.6 pad_add_fusion.start_ref
  16.3 0.9 slice.48
  17.2 1.4 %collective-permute-start.3 = (bf16[16,4,192]{2,1,0:T(4,128)(2,1)S(1)}, bf16[16,4,192]{2,1,0:T(4,128)(2,1)S(1)}, u32[]{:S(2)}, u32[]{:S(2)}) collective-permute-start(bf16[16,4,192]{2,1,0:T(4,128)(2,1)S(1)} %pad_maximum_fusion.6), channel_id=1, source_target_pairs={{0,7},{1,0},{2,1},{3,2},{4,3},{5,4},{6,5},{7,6},{8,15},{9,8},{10,9... | collective-permute-start | bytes 73736 | tf_op jit(solution)/shard_map/ppermute | solution.py:539
  18.6 0.6 collective-permute-done
  19.2 0.7 collective-permute-start.1
  20.2 0.7 pad_maximum_fusion.3.g_ref
  20.9 0.6 collective-permute-done.1
  21.5 0.7 pad_maximum_fusion.2.x_ref
  22.2 8.0 %both1.1 = (bf16[16,16,192]{2,1,0:T(8,128)(2,1)}, bf16[16,16,192]{2,1,0:T(8,128)(2,1)}, bf16[640,768]{1,0:T(8,128)(2,1)}) custom-call(s32[2]{0:T(128)} %pad_add_fusion.start_ref, bf16[16,16,192]{2,1,0:T(8,128)(2,1)} %pad_maximum_fusion.2.x_ref, bf16[16,16,192]{2,1,0:T(8,128)(2,1)} %pad_maximum_fusion.3.g_ref, f32[2,192]{1,0:T(2,128)} %refs_0_.5, ...), custom_call_target="tpu_custom_call" | custom-call | tf_op jit(solution)/shard_map/both1/pallas_call | solution.py:355
  30.2 0.8 slice.60
  30.9 1.6 %collective-permute-start.6 = (bf16[4,16,192]{2,1,0:T(8,128)(2,1)S(1)}, bf16[4,16,192]{2,1,0:T(8,128)(2,1)S(1)}, u32[]{:S(2)}, u32[]{:S(2)}) collective-permute-start(bf16[4,16,192]{2,1,0:T(8,128)(2,1)S(1)} %slice.60), channel_id=1, source_target_pairs={{0,8},{8,16},{16,24},{24,0},{1,9},{9,17},{17,25},{25,1},{2,10},{10... | collective-permute-start | bytes 73736 | tf_op jit(solution)/shard_map/ppermute | solution.py:539
  32.5 0.8 slice.56
  33.3 0.9 slice.57
  34.2 0.9 slice.61
  35.1 1.9 %collective-permute-done.6 = bf16[4,16,192]{2,1,0:T(8,128)(2,1)S(1)} collective-permute-done((bf16[4,16,192]{2,1,0:T(8,128)(2,1)S(1)}, bf16[4,16,192]{2,1,0:T(8,128)(2,1)S(1)}, u32[]{:S(2)}, u32[]{:S(2)}) %collective-permute-start.6) | collective-permute-done | bytes 24608 | tf_op jit(solution)/shard_map/ppermute | solution.py:539
  37.1 3.7 %collective-permute-done.4 = bf16[4,16,192]{2,1,0:T(8,128)(2,1)S(1)} collective-permute-done((bf16[4,16,192]{2,1,0:T(8,128)(2,1)S(1)}, bf16[4,16,192]{2,1,0:T(8,128)(2,1)S(1)}, u32[]{:S(2)}, u32[]{:S(2)}) %collective-permute-start.4) | collective-permute-done | bytes 24608 | tf_op jit(solution)/shard_map/ppermute | solution.py:539
  40.8 0.2 collective-permute-start.5
  41.1 0.2 collective-permute-done.7
  41.3 0.7 fusion.g_ref
  42.0 7.3 %bwd0.1 = (bf16[16,16,192]{2,1,0:T(8,128)(2,1)}, bf16[640,768]{1,0:T(8,128)(2,1)}) custom-call(bf16[16,16,192]{2,1,0:T(8,128)(2,1)} %x_ref.3, bf16[16,16,192]{2,1,0:T(8,128)(2,1)} %fusion.g_ref, bf16[256,576]{1,0:T(8,128)(2,1)} %get-tuple-element.42.packed_ref, bf16[256,192]{1,0:T(8,128)(2,1)} %get-tuple-element.43.mixed_ref, ...), custom_call_target="tpu_custom_call" | custom-call | tf_op jit(solution)/shard_map/bwd0/pallas_call | solution.py:382
  49.3 44.7 %sum_all.1.s_ref = bf16[1280,768]{1,0:T(8,128)(2,1)} custom-call(bf16[640,768]{1,0:T(8,128)(2,1)} %get-tuple-element.48.one_ref, bf16[640,768]{1,0:T(8,128)(2,1)} %get-tuple-element.49.two_ref), custom_call_target="tpu_custom_call" | custom-call | tf_op jit(solution)/shard_map/sum_all/pallas_call | solution.py:479
  94.0 4.1 %unpack.1 = (f32[2,192]{1,0:T(2,128)}, f32[2,192]{1,0:T(2,128)}, f32[2,192,576]{2,1,0:T(8,128)}, f32[2,576]{1,0:T(2,128)}, f32[2,6,225]{2,1,0:T(8,128)}, /*index...) custom-call(bf16[1280,768]{1,0:T(8,128)(2,1)} %sum_all.1.s_ref), custom_call_target="tpu_custom_call" | custom-call | tf_op jit(solution)/shard_map/unpack/pallas_call | solution.py:526
  98.1 1.3 %copy.36 = f32[2,6,225]{2,0,1:T(2,128)} copy(f32[2,6,225]{2,1,0:T(8,128)} %get-tuple-element.69) | data formatting | bytes 21600
  99.4 2.9 %copy.37 = f32[2,768,192]{1,2,0:T(8,128)} copy(f32[2,768,192]{2,1,0:T(8,128)} %get-tuple-element.76) | data formatting | bytes 2359296
  102.3 0.7 fusion.1
  (14 shorter events, 0.5 us)
Async XLA Ops:
  1.4 15.8 %collective-permute-start.2 = (bf16[4,16,192]{2,1,0:T(8,128)(2,1)S(1)}, bf16[4,16,192]{2,1,0:T(8,128)(2,1)S(1)}, u32[]{:S(2)}, u32[]{:S(2)}) collective-permute-start(bf16[4,16,192]{2,1,0:T(8,128)(2,1)S(1)} %slice.53), channel_id=1, source_target_pairs={{0,24},{8,0},{16,8},{24,16},{1,25},{9,1},{17,9},{25,17},{2,26},{10... | collective-permute-start | bytes 73736 | tf_op jit(solution)/shard_map/ppermute | solution.py:539
  7.8 8.5 %copy-start = (bf16[16,16,192]{2,1,0:T(8,128)(2,1)S(1)}, bf16[16,16,192]{2,1,0:T(8,128)(2,1)}, u32[]{:S(2)}) copy-start(bf16[16,16,192]{2,1,0:T(8,128)(2,1)} %param.16) | copy-start | bytes 294916
  15.2 3.9 %collective-permute-start = (bf16[4,16,192]{2,1,0:T(8,128)(2,1)S(1)}, bf16[4,16,192]{2,1,0:T(8,128)(2,1)S(1)}, u32[]{:S(2)}, u32[]{:S(2)}) collective-permute-start(bf16[4,16,192]{2,1,0:T(8,128)(2,1)S(1)} %slice.49), channel_id=1, source_target_pairs={{0,24},{8,0},{16,8},{24,16},{1,25},{9,1},{17,9},{25,17},{2,26},{10... | collective-permute-start | bytes 73736 | tf_op jit(solution)/shard_map/ppermute | solution.py:539
  17.2 3.0 %collective-permute-start.3 = (bf16[16,4,192]{2,1,0:T(4,128)(2,1)S(1)}, bf16[16,4,192]{2,1,0:T(4,128)(2,1)S(1)}, u32[]{:S(2)}, u32[]{:S(2)}) collective-permute-start(bf16[16,4,192]{2,1,0:T(4,128)(2,1)S(1)} %pad_maximum_fusion.6), channel_id=1, source_target_pairs={{0,7},{1,0},{2,1},{3,2},{4,3},{5,4},{6,5},{7,6},{8,15},{9,8},{10,9... | collective-permute-start | bytes 73736 | tf_op jit(solution)/shard_map/ppermute | solution.py:539
  19.2 2.3 %collective-permute-start.1 = (bf16[16,4,192]{2,1,0:T(4,128)(2,1)S(1)}, bf16[16,4,192]{2,1,0:T(4,128)(2,1)S(1)}, u32[]{:S(2)}, u32[]{:S(2)}) collective-permute-start(bf16[16,4,192]{2,1,0:T(4,128)(2,1)S(1)} %pad_maximum_fusion.7), channel_id=1, source_target_pairs={{0,7},{1,0},{2,1},{3,2},{4,3},{5,4},{6,5},{7,6},{8,15},{9,8},{10,9... | collective-permute-start | bytes 73736 | tf_op jit(solution)/shard_map/ppermute | solution.py:539
  30.9 6.0 %collective-permute-start.6 = (bf16[4,16,192]{2,1,0:T(8,128)(2,1)S(1)}, bf16[4,16,192]{2,1,0:T(8,128)(2,1)S(1)}, u32[]{:S(2)}, u32[]{:S(2)}) collective-permute-start(bf16[4,16,192]{2,1,0:T(8,128)(2,1)S(1)} %slice.60), channel_id=1, source_target_pairs={{0,8},{8,16},{16,24},{24,0},{1,9},{9,17},{17,25},{25,1},{2,10},{10... | collective-permute-start | bytes 73736 | tf_op jit(solution)/shard_map/ppermute | solution.py:539
  35.1 5.7 %collective-permute-start.4 = (bf16[4,16,192]{2,1,0:T(8,128)(2,1)S(1)}, bf16[4,16,192]{2,1,0:T(8,128)(2,1)S(1)}, u32[]{:S(2)}, u32[]{:S(2)}) collective-permute-start(bf16[4,16,192]{2,1,0:T(8,128)(2,1)S(1)} %slice.56), channel_id=1, source_target_pairs={{0,8},{8,16},{16,24},{24,0},{1,9},{9,17},{17,25},{25,1},{2,10},{10... | collective-permute-start | bytes 73736 | tf_op jit(solution)/shard_map/ppermute | solution.py:539
  37.0 4.3 %collective-permute-start.7 = (bf16[16,4,192]{2,1,0:T(4,128)(2,1)S(1)}, bf16[16,4,192]{2,1,0:T(4,128)(2,1)S(1)}, u32[]{:S(2)}, u32[]{:S(2)}) collective-permute-start(bf16[16,4,192]{2,1,0:T(4,128)(2,1)S(1)} %pad_maximum_fusion.4), channel_id=1, source_target_pairs={{0,1},{1,2},{2,3},{3,4},{4,5},{5,6},{6,7},{7,0},{8,9},{9,10},{10,1... | collective-permute-start | bytes 73736 | tf_op jit(solution)/shard_map/ppermute | solution.py:539
  40.8 61.5 %collective-permute-start.5 = (bf16[16,4,192]{2,1,0:T(4,128)(2,1)S(1)}, bf16[16,4,192]{2,1,0:T(4,128)(2,1)S(1)}, u32[]{:S(2)}, u32[]{:S(2)}) collective-permute-start(bf16[16,4,192]{2,1,0:T(4,128)(2,1)S(1)} %pad_maximum_fusion.5), channel_id=1, source_target_pairs={{0,1},{1,2},{2,3},{3,4},{4,5},{5,6},{6,7},{7,0},{8,9},{9,10},{10,1... | collective-permute-start | bytes 73736 | tf_op jit(solution)/shard_map/ppermute | solution.py:539
where the time goes:
time: 104 us; the launch traced here: 103 us
  Pallas kernels  68.5 us (66%)
  local copies, waits for them, and re-layouts  13.5 us (13%)
  starting transfers between devices  9.58 us (9%)
  waiting for transfers between devices  7.12 us (7%)
  other arithmetic  3.57 us (3%)
    pallas_call x1, Pallas kernels, sum_all(): pl.pallas_call(body, name='sum_all', out_shape=shape_of((rows, width), BF...  44.7 us
    ppermute x8, starting transfers between devices, from_behind(): return lax.ppermute(value, axis, pairs)  9.58 us
    pallas_call x1, Pallas kernels, second_both(): pl.pallas_call(body, name='both1', grid=(1,), out_shape=outs, in_specs=[p...  7.97 us
    unnamed x6, local copies, waits for them, and re-layouts  7.76 us
    pallas_call x1, Pallas kernels, first_backward(): pl.pallas_call(body, name='bwd0', grid=(1,), out_shape=outs, in_specs=[wh...  7.31 us
    ppermute x8, waiting for transfers between devices, from_behind(): return lax.ppermute(value, axis, pairs)  7.12 us
    pallas_call x1, Pallas kernels, first_forward(): pl.pallas_call(body, name='fwd0', grid=(1,), out_shape=outs, in_specs=[wh...  4.41 us
    pallas_call x1, Pallas kernels, unpack(): pl.pallas_call(body, name='unpack', grid=(1,), out_shape=outs, in_specs=[...  4.09 us
  transfers between devices with their start and end apart: 8, of which 6 were waited for; matrix products, arithmetic and copies ran while one was open for 14% of the time, Pallas kernels for 59%

commit v1 on v0

--- a/solution.py
+++ b/solution.py
@@ -102,7 +102,7 @@
     pick = (lanes == cell_code(cells, 0, (cells, 128))).astype(BF16)
     outs = []
     for h in range(heads):
-        row = jnp.concatenate([rel[h : h + 1], jnp.zeros((1, width - span * span), F32)], axis=1)
+        row = jnp.concatenate([rel[h], jnp.zeros((1, width - span * span), F32)], axis=1)
         row = jnp.broadcast_to(row, (WIN, width))
         rolled = [
             pltpu.roll(row, (span * y - middle) % width, 1, stride=1, stride_axis=0)[:, :128]
@@ -199,7 +199,7 @@
     pre = mm(normed2, w["wup"][0]) + w["bup"][...]
     half = 0.5 * (1.0 + lax.erf(pre * (2.0**-0.5)))
     hidden = (pre * half).astype(BF16)
-    out = (mid32 + mm(hidden, w["wdown"][0]) + w["bdown"][...]).astype(BF16)
+    out = (mid32 + mm_nt(hidden, w["wdown"][0]) + w["bdown"][...]).astype(BF16)
     return out, (packed, mixed, mid, pre)
 
 
@@ -216,7 +216,7 @@
     hidden = (pre * half).astype(BF16)
     grads_ref[2 * channels : 3 * channels, :] = mm_tn(g16, hidden).astype(BF16)
     light_ref[3:4, :channels] = jnp.sum(g, axis=0, keepdims=True)
-    dpre = rnd(mm_nt(g16, w["wdown"][0])) * slope
+    dpre = rnd(mm(g16, w["wdown"][0])) * slope
     light_ref[0:1, : dpre.shape[1]] = jnp.sum(dpre, axis=0, keepdims=True)
     dpre16 = dpre.astype(BF16)
     mid32 = mid.astype(F32)
@@ -267,13 +267,16 @@
 
 
 KEYS = ("ng", "nb", "wqkv", "bqkv", "rel", "wproj", "bproj", "mg", "mb", "wup", "bup", "wdown", "bdown")
-MATRICES = ("wqkv", "rel", "wproj", "wup", "wdown")
+MATRICES = ("wqkv", "wproj", "wup", "wdown")
 
 
 def weight_view(refs, block):
     view = {}
     for key, ref in zip(KEYS, refs):
-        view[key] = ref if key in MATRICES else ref.at[block : block + 1, :]
+        if key == "rel":
+            view[key] = [ref[h, block : block + 1, :] for h in range(ref.shape[0])]
+        else:
+            view[key] = ref if key in MATRICES else ref.at[block : block + 1, :]
     return view
 
 
@@ -283,7 +286,7 @@
         if key in MATRICES:
             specs.append(pl.BlockSpec((1,) + member.shape[1:], lambda i: (block, 0, 0)))
         else:
-            specs.append(pl.BlockSpec(member.shape, lambda i: (0, 0)))
+            specs.append(whole(member.shape))
     return specs
 
 
@@ -297,7 +300,7 @@
 
 def first_forward(imagery, params):
     height, breadth, channels = imagery.shape
-    heads = params[4].shape[1]
+    heads = params[4].shape[0]
     tokens = height * breadth
     mlp = params[9].shape[2]
 
@@ -305,7 +308,7 @@
         w = weight_view(refs[: len(KEYS)], 0)
         out_ref, packed_ref, mixed_ref, mid_ref, pre_ref, pos_ref = refs[len(KEYS) :]
         x = load_windows(x_ref, height, breadth)
-        position = position_stack(w["rel"][0], heads)
+        position = position_stack(w["rel"], heads)
         pos_ref[...] = position
         out, saved = forward(x, w, position, None, heads)
         store_windows(out_ref, out.astype(F32), height, breadth)
@@ -332,14 +335,14 @@
 
 def second_both(moved, grad, start, params, total_rows, total_cols, grad_rows):
     height, breadth, channels = moved.shape
-    heads = params[4].shape[1]
+    heads = params[4].shape[0]
     width = params[9].shape[2]
 
     def body(start_ref, x_ref, g_ref, *refs):
         w = weight_view(refs[: len(KEYS)], 1)
         out_ref, dx_ref, grads_ref, light_ref = refs[len(KEYS) :]
         x = load_windows(x_ref, height, breadth)
-        position = position_stack(w["rel"][0], heads)
+        position = position_stack(w["rel"], heads)
         masks = zone_masks(start_ref, height, breadth, total_rows, total_cols, heads)
         out, saved = forward(x, w, position, masks, heads)
         store_windows(out_ref, out.astype(F32), height, breadth)
@@ -366,7 +369,7 @@
 
 def first_backward(imagery, grad, saved, params, grad_rows):
     height, breadth, channels = imagery.shape
-    heads = params[4].shape[1]
+    heads = params[4].shape[0]
     width = params[9].shape[2]
 
     def body(x_ref, g_ref, packed_ref, mixed_ref, mid_ref, pre_ref, pos_ref, *refs):
@@ -396,8 +399,11 @@
     block_rows, width = grads_one.shape
     rows = 2 * block_rows
     half = width // 2
-    part = rows // nq
-    piece = part // nz
+    unit = nq * nz * 16
+    count = rows // unit
+    part = unit // nq
+    piece = 16
+    per_chunk = 2 * nq + 2 * nz - 1
 
     def body(one_ref, two_ref, out_ref, buf0, acc, buf1, acc1, buf2, send, recv):
         z = lax.axis_index("rows")
@@ -413,8 +419,11 @@
         for peer in [partner] + across + along:
             pl.semaphore_signal(barrier, inc=1, device_id=peer, device_id_type=MESH)
         pl.semaphore_wait(barrier, nq + nz - 1)
-
-        def copy(src, dst, index, peer):
+        lanes = pl.ds(mine, half)
+        pending = {}
+
+        def copy(chunk, slot, src, dst, peer):
+            index = chunk * per_chunk + slot
             c = pltpu.make_async_remote_copy(
                 src_ref=src,
                 dst_ref=dst,
@@ -424,57 +433,83 @@
                 device_id_type=MESH,
             )
             c.start()
-            return c
-
-        sem = 0
-        copies = []
-        for b, ref in enumerate((one_ref, two_ref)):
-            copies.append(
-                copy(ref.at[:, pl.ds(other, half)], buf0.at[pl.ds(b * block_rows, block_rows), :], sem, partner)
-            )
-            sem += 1
-        for b, ref in enumerate((one_ref, two_ref)):
-            copies[b].wait()
-            at = pl.ds(b * block_rows, block_rows)
-            acc[at, :] = (ref[:, pl.ds(mine, half)].astype(F32) + buf0[at, :].astype(F32)).astype(BF16)
-        copies = []
-        for d in range(1, nq):
-            to = pl.multiple_of(lax.rem(q + d, nq) * part, 16)
-            copies.append(copy(acc.at[pl.ds(to, part), :], buf1.at[d - 1], sem, across[d - 1]))
-            sem += 1
-        total = acc[pl.ds(pl.multiple_of(q * part, 16), part), :].astype(F32)
-        for d in range(1, nq):
-            copies[d - 1].wait()
-            total = total + buf1[d - 1].astype(F32)
-        acc1[...] = total.astype(BF16)
-        copies = []
-        for d in range(1, nz):
-            to = pl.multiple_of(lax.rem(z + d, nz) * piece, 16)
-            copies.append(copy(acc1.at[pl.ds(to, piece), :], buf2.at[d - 1], sem, along[d - 1]))
-            sem += 1
-        total = acc1[pl.ds(pl.multiple_of(z * piece, 16), piece), :].astype(F32)
-        for d in range(1, nz):
-            copies[d - 1].wait()
-            total = total + buf2[d - 1].astype(F32)
-        lanes = pl.ds(mine, half)
-        own = pl.ds(pl.multiple_of(q * part + z * piece, 16), piece)
-        out_ref[own, lanes] = total.astype(BF16)
-        copies = []
-        for d in range(1, nz):
-            copies.append(copy(out_ref.at[own, lanes], out_ref.at[own, lanes], sem, along[d - 1]))
-            sem += 1
-        for c in copies:
-            c.wait()
-        copies = []
-        own = pl.ds(pl.multiple_of(q * part, 16), part)
-        for d in range(1, nq):
-            copies.append(copy(out_ref.at[own, lanes], out_ref.at[own, lanes], sem, across[d - 1]))
-            sem += 1
-        for c in copies:
-            c.wait()
-        copy(out_ref.at[:, lanes], out_ref.at[:, lanes], sem, partner).wait()
-
-    sems = 2 + 2 * (nq - 1) + 2 * (nz - 1) + 1
+            pending.setdefault(chunk, []).append(c)
+
+        def finish(chunk):
+            for c in pending.pop(chunk):
+                c.wait()
+
+        def pieces(chunk):
+            low, high = chunk * unit, (chunk + 1) * unit
+            found = []
+            for b, ref in ((1, two_ref), (0, one_ref)):
+                base = (1 - b) * block_rows
+                lo, hi = max(low, base), min(high, base + block_rows)
+                if lo < hi:
+                    found.append((ref, lo - base, lo - low, hi - lo))
+            return found
+
+        def stage0(c):
+            for place, (ref, at, to, size) in enumerate(pieces(c)):
+                copy(
+                    c,
+                    place,
+                    ref.at[at : at + size, pl.ds(other, half)],
+                    buf0.at[c * unit + to : c * unit + to + size, :],
+                    partner,
+                )
+
+        def stage1(c):
+            finish(c)
+            for ref, at, to, size in pieces(c):
+                where = slice(c * unit + to, c * unit + to + size)
+                acc[where, :] = (
+                    ref[at : at + size, lanes].astype(F32) + buf0[where, :].astype(F32)
+                ).astype(BF16)
+            for d in range(1, nq):
+                to = pl.multiple_of(c * unit + lax.rem(q + d, nq) * part, 16)
+                copy(c, 1 + d, acc.at[pl.ds(to, part), :], buf1.at[c, d - 1], across[d - 1])
+
+        def stage2(c):
+            finish(c)
+            total = acc[pl.ds(pl.multiple_of(c * unit + q * part, 16), part), :].astype(F32)
+            for d in range(1, nq):
+                total = total + buf1[c, d - 1].astype(F32)
+            acc1[c] = total.astype(BF16)
+            for d in range(1, nz):
+                to = pl.multiple_of(lax.rem(z + d, nz) * piece, 16)
+                copy(c, nq + d, acc1.at[c, pl.ds(to, piece), :], buf2.at[c, d - 1], along[d - 1])
+
+        def stage3(c):
+            finish(c)
+            total = acc1[c, pl.ds(pl.multiple_of(z * piece, 16), piece), :].astype(F32)
+            for d in range(1, nz):
+                total = total + buf2[c, d - 1].astype(F32)
+            own = pl.ds(pl.multiple_of(c * unit + q * part + z * piece, 16), piece)
+            out_ref[own, lanes] = total.astype(BF16)
+            for d in range(1, nz):
+                copy(c, nq + nz - 1 + d, out_ref.at[own, lanes], out_ref.at[own, lanes], along[d - 1])
+
+        def stage4(c):
+            finish(c)
+            own = pl.ds(pl.multiple_of(c * unit + q * part, 16), part)
+            for d in range(1, nq):
+                copy(c, nq + 2 * nz - 2 + d, out_ref.at[own, lanes], out_ref.at[own, lanes], across[d - 1])
+
+        def stage5(c):
+            finish(c)
+            own = slice(c * unit, (c + 1) * unit)
+            copy(c, 2 * nq + 2 * nz - 2, out_ref.at[own, lanes], out_ref.at[own, lanes], partner)
+
+        stages = (stage1, stage2, stage3, stage4, stage5, finish)
+        for c in range(count):
+            stage0(c)
+        for tick in range(count + len(stages) - 1):
+            for c in range(count):
+                if 0 <= tick - c < len(stages):
+                    stages[tick - c](c)
+
+    sems = per_chunk * count
     vmem = pl.BlockSpec(memory_space=pltpu.VMEM)
     return pl.pallas_call(
         body,
@@ -485,9 +520,9 @@
         scratch_shapes=[
             pltpu.VMEM((rows, half), BF16),
             pltpu.VMEM((rows, half), BF16),
-            pltpu.VMEM((max(nq - 1, 1), part, half), BF16),
-            pltpu.VMEM((part, half), BF16),
-            pltpu.VMEM((max(nz - 1, 1), piece, half), BF16),
+            pltpu.VMEM((count, max(nq - 1, 1), part, half), BF16),
+            pltpu.VMEM((count, part, half), BF16),
+            pltpu.VMEM((count, max(nz - 1, 1), piece, half), BF16),
             pltpu.SemaphoreType.DMA((sems,)),
             pltpu.SemaphoreType.DMA((sems,)),
         ],
@@ -497,13 +532,13 @@
 
 def unpack(summed, params, factor):
     channels = params[0].shape[1]
-    heads, offsets = params[4].shape[1:]
+    heads, _, offsets = params[4].shape
     block_rows = summed.shape[0] // 2
 
     def body(s_ref, *outs):
         o = dict(zip(KEYS, outs))
         for b in range(2):
-            at = b * block_rows
+            at = (1 - b) * block_rows
 
             def rows(low, count):
                 return s_ref[at + low : at + low + count, :].astype(F32) * factor
@@ -512,7 +547,7 @@
             o["wqkv"][b] = top[:, : 3 * channels]
             o["wproj"][b] = top[:, 3 * channels :]
             o["wup"][b] = rows(channels, channels)
-            o["wdown"][b] = rows(2 * channels, channels).T
+            o["wdown"][b] = rows(2 * channels, channels)
             light = rows(3 * channels, 16)
             o["bup"][b : b + 1, :] = light[0:1, :]
             o["bqkv"][b : b + 1, :] = light[1:2, : 3 * channels]
@@ -520,7 +555,8 @@
             for place, key in enumerate(("ng", "nb", "mg", "mb")):
                 o[key][b : b + 1, :] = light[2:3, place * channels : (place + 1) * channels]
             o["bdown"][b : b + 1, :] = light[3:4, :channels]
-            o["rel"][b] = light[4 : 4 + heads, :offsets]
+            for h in range(heads):
+                o["rel"][h, b : b + 1, :] = light[4 + h : 5 + h, :offsets]
 
     outs = [shape_of(member.shape, F32) for member in params]
     return pl.pallas_call(
@@ -566,6 +602,9 @@
     nc = lax.axis_size("cols")
     total_rows = height * nz
     total_cols = breadth * nc
+    params = list(params)
+    params[4] = jnp.swapaxes(params[4], 0, 1)
+    params[11] = jnp.swapaxes(params[11], 1, 2)
     start = jnp.stack(
         [lax.axis_index("rows") * height, lax.axis_index("cols") * breadth]
     ).astype(jnp.int32)
@@ -579,6 +618,9 @@
     back_one, grads_one = first_backward(imagery, retreat(back_two), saved, params, grad_rows)
     summed = sum_all(grads_one, grads_two, nz, nc // 2)
     merged = unpack(summed, params, float(total_rows * total_cols) ** (-0.5))
+    merged = list(merged)
+    merged[4] = jnp.swapaxes(merged[4], 0, 1)
+    merged[11] = jnp.swapaxes(merged[11], 1, 2)
     return (output, back_one) + tuple(merged)
 
 

time: 104 us -> 93.4 us (0.90)
  local copies, waits for them, and re-layouts: 13.5 us -> 5.82 us
  Pallas kernels: 68.5 us -> 66 us
    unnamed x6 -> x2, local copies, waits for them, and re-layouts: 7.76 us -> 0.01 us
    pallas_call x1, Pallas kernels: 44.7 us -> 42.8 us  [sum_all(): pl.pallas_call(body, name='sum_all', out_shape=shape_of((rows, width), BF...]
  transfers between devices with their start and end apart: 8 -> 8, of which waited for: 6 -> 6; matrix products, arithmetic and copies ran while one was open for 14% -> 7% of each run, Pallas kernels for 59% -> 63%
where the time goes in v1:
time: 93.4 us; the launch traced here: 92.9 us
  Pallas kernels  66 us (71%)
  starting transfers between devices  9.57 us (10%)
  waiting for transfers between devices  7.13 us (8%)
  local copies, waits for them, and re-layouts  5.82 us (6%)
  other arithmetic  3.57 us (4%)
    pallas_call x1, Pallas kernels, sum_all(): pl.pallas_call(body, name='sum_all', out_shape=shape_of((rows, width), BF...  42.8 us
    ppermute x8, starting transfers between devices, from_behind(): return lax.ppermute(value, axis, pairs)  9.57 us
    pallas_call x1, Pallas kernels, second_both(): pl.pallas_call(body, name='both1', grid=(1,), out_shape=outs, in_specs=[p...  7.93 us
    pallas_call x1, Pallas kernels, first_backward(): pl.pallas_call(body, name='bwd0', grid=(1,), out_shape=outs, in_specs=[wh...  7.27 us
    ppermute x8, waiting for transfers between devices, from_behind(): return lax.ppermute(value, axis, pairs)  7.13 us
    pallas_call x1, Pallas kernels, first_forward(): pl.pallas_call(body, name='fwd0', grid=(1,), out_shape=outs, in_specs=[wh...  4.38 us
    pallas_call x1, Pallas kernels, unpack(): pl.pallas_call(body, name='unpack', grid=(1,), out_shape=outs, in_specs=[...  3.62 us
    concatenate x8, other arithmetic, along_axis(): jnp.concatenate([kept, arrived] if direction < 0 else [arrived, kept], ax...  2.94 us
  transfers between devices with their start and end apart: 8, of which 6 were waited for; matrix products, arithmetic and copies ran while one was open for 7% of the time, Pallas kernels for 63%

profile of v1, /device:TPU:0, one launch (start us, length us, event | category | flops | bytes accessed | tf_op | source)
XLA Modules:
  0.0 92.9 jit_solution(3290623412011303483)
XLA Ops:
  0.7 0.8 slice.53
  1.5 5.1 %collective-permute-start.2 = (bf16[4,16,192]{2,1,0:T(8,128)(2,1)S(1)}, bf16[4,16,192]{2,1,0:T(8,128)(2,1)S(1)}, u32[]{:S(2)}, u32[]{:S(2)}) collective-permute-start(bf16[4,16,192]{2,1,0:T(8,128)(2,1)S(1)} %slice.53), channel_id=1, source_target_pairs={{0,24},{8,0},{16,8},{24,16},{1,25},{9,1},{17,9},{25,17},{2,26},{10... | collective-permute-start | bytes 73736 | tf_op jit(solution)/shard_map/ppermute | solution.py:575
  6.6 4.4 %fwd0.1 = (bf16[16,16,192]{2,1,0:T(8,128)(2,1)}, bf16[256,576]{1,0:T(8,128)(2,1)}, bf16[256,192]{1,0:T(8,128)(2,1)}, bf16[256,192]{1,0:T(8,128)(2,1)}, f32[256,768]{1,0:T(8,128)}, /*index=5*/f32[384,64]{1,0:T(8,128)}) custom-call(bf16[16,16,192]{2,1,0:T(8,128)(2,1)} %x_ref.3, f32[2,192]{1,0:T(2,128)} %refs_0_.5, f32[2,192]{1,0:T(2,128)} %refs_1_.5, ...), custom_call_target="tpu_custom_call" | custom-call | tf_op jit(solution)/shard_map/fwd0/pallas_call | solution.py:326
  10.9 0.8 slice.49
  11.7 0.4 collective-permute-start
  12.2 0.6 pad_add_fusion.start_ref
  12.8 0.9 slice.48
  13.7 0.0 collective-permute-done.2
  13.7 1.4 %collective-permute-start.3 = (bf16[16,4,192]{2,1,0:T(4,128)(2,1)S(1)}, bf16[16,4,192]{2,1,0:T(4,128)(2,1)S(1)}, u32[]{:S(2)}, u32[]{:S(2)}) collective-permute-start(bf16[16,4,192]{2,1,0:T(4,128)(2,1)S(1)} %pad_maximum_fusion.6), channel_id=1, source_target_pairs={{0,7},{1,0},{2,1},{3,2},{4,3},{5,4},{6,5},{7,6},{8,15},{9,8},{10,9... | collective-permute-start | bytes 73736 | tf_op jit(solution)/shard_map/ppermute | solution.py:575
  15.1 0.6 collective-permute-done
  15.6 0.7 collective-permute-start.1
  16.5 0.2 collective-permute-done.3
  16.7 0.7 pad_maximum_fusion.3.g_ref
  17.4 0.6 collective-permute-done.1
  18.0 0.7 pad_maximum_fusion.2.x_ref
  18.7 7.9 %both1.1 = (bf16[16,16,192]{2,1,0:T(8,128)(2,1)}, bf16[16,16,192]{2,1,0:T(8,128)(2,1)}, bf16[640,768]{1,0:T(8,128)(2,1)}) custom-call(s32[2]{0:T(128)} %pad_add_fusion.start_ref, bf16[16,16,192]{2,1,0:T(8,128)(2,1)} %pad_maximum_fusion.2.x_ref, bf16[16,16,192]{2,1,0:T(8,128)(2,1)} %pad_maximum_fusion.3.g_ref, f32[2,192]{1,0:T(2,128)} %refs_0_.5, ...), custom_call_target="tpu_custom_call" | custom-call | tf_op jit(solution)/shard_map/both1/pallas_call | solution.py:358
  26.6 0.8 slice.60
  27.4 1.6 %collective-permute-start.6 = (bf16[4,16,192]{2,1,0:T(8,128)(2,1)S(1)}, bf16[4,16,192]{2,1,0:T(8,128)(2,1)S(1)}, u32[]{:S(2)}, u32[]{:S(2)}) collective-permute-start(bf16[4,16,192]{2,1,0:T(8,128)(2,1)S(1)} %slice.60), channel_id=1, source_target_pairs={{0,8},{8,16},{16,24},{24,0},{1,9},{9,17},{17,25},{25,1},{2,10},{10... | collective-permute-start | bytes 73736 | tf_op jit(solution)/shard_map/ppermute | solution.py:575
  28.9 0.8 slice.56
  29.7 0.9 slice.57
  30.6 0.9 slice.61
  31.5 0.0 collective-permute-start.4
  31.5 1.9 %collective-permute-done.6 = bf16[4,16,192]{2,1,0:T(8,128)(2,1)S(1)} collective-permute-done((bf16[4,16,192]{2,1,0:T(8,128)(2,1)S(1)}, bf16[4,16,192]{2,1,0:T(8,128)(2,1)S(1)}, u32[]{:S(2)}, u32[]{:S(2)}) %collective-permute-start.6) | collective-permute-done | bytes 24608 | tf_op jit(solution)/shard_map/ppermute | solution.py:575
  33.4 0.1 collective-permute-start.7
  33.5 3.7 %collective-permute-done.4 = bf16[4,16,192]{2,1,0:T(8,128)(2,1)S(1)} collective-permute-done((bf16[4,16,192]{2,1,0:T(8,128)(2,1)S(1)}, bf16[4,16,192]{2,1,0:T(8,128)(2,1)S(1)}, u32[]{:S(2)}, u32[]{:S(2)}) %collective-permute-start.4) | collective-permute-done | bytes 24608 | tf_op jit(solution)/shard_map/ppermute | solution.py:575
  37.2 0.2 collective-permute-start.5
  37.5 0.2 collective-permute-done.7
  37.7 0.7 fusion.g_ref
  38.4 7.3 %bwd0.1 = (bf16[16,16,192]{2,1,0:T(8,128)(2,1)}, bf16[640,768]{1,0:T(8,128)(2,1)}) custom-call(bf16[16,16,192]{2,1,0:T(8,128)(2,1)} %x_ref.3, bf16[16,16,192]{2,1,0:T(8,128)(2,1)} %fusion.g_ref, bf16[256,576]{1,0:T(8,128)(2,1)} %get-tuple-element.42.packed_ref, bf16[256,192]{1,0:T(8,128)(2,1)} %get-tuple-element.43.mixed_ref, ...), custom_call_target="tpu_custom_call" | custom-call | tf_op jit(solution)/shard_map/bwd0/pallas_call | solution.py:385
  45.7 42.8 %sum_all.1.s_ref = bf16[1280,768]{1,0:T(8,128)(2,1)} custom-call(bf16[640,768]{1,0:T(8,128)(2,1)} %get-tuple-element.48.one_ref, bf16[640,768]{1,0:T(8,128)(2,1)} %get-tuple-element.49.two_ref), custom_call_target="tpu_custom_call" | custom-call | tf_op jit(solution)/shard_map/sum_all/pallas_call | solution.py:514
  88.5 3.6 %unpack.1 = (f32[2,192]{1,0:T(2,128)}, f32[2,192]{1,0:T(2,128)}, f32[2,192,576]{2,1,0:T(8,128)}, f32[2,576]{1,0:T(2,128)}, f32[6,2,225]{2,1,0:T(2,128)}, /*index...) custom-call(bf16[1280,768]{1,0:T(8,128)(2,1)} %sum_all.1.s_ref), custom_call_target="tpu_custom_call" | custom-call | tf_op jit(solution)/shard_map/unpack/pallas_call | solution.py:562
  92.2 0.7 fusion.1
  (10 shorter events, 0.2 us)
Async XLA Ops:
  0.6 12.1 %copy-start = (bf16[16,16,192]{2,1,0:T(8,128)(2,1)S(1)}, bf16[16,16,192]{2,1,0:T(8,128)(2,1)}, u32[]{:S(2)}) copy-start(bf16[16,16,192]{2,1,0:T(8,128)(2,1)} %param.16) | copy-start | bytes 294916
  1.5 12.2 %collective-permute-start.2 = (bf16[4,16,192]{2,1,0:T(8,128)(2,1)S(1)}, bf16[4,16,192]{2,1,0:T(8,128)(2,1)S(1)}, u32[]{:S(2)}, u32[]{:S(2)}) collective-permute-start(bf16[4,16,192]{2,1,0:T(8,128)(2,1)S(1)} %slice.53), channel_id=1, source_target_pairs={{0,24},{8,0},{16,8},{24,16},{1,25},{9,1},{17,9},{25,17},{2,26},{10... | collective-permute-start | bytes 73736 | tf_op jit(solution)/shard_map/ppermute | solution.py:575
  11.7 3.9 %collective-permute-start = (bf16[4,16,192]{2,1,0:T(8,128)(2,1)S(1)}, bf16[4,16,192]{2,1,0:T(8,128)(2,1)S(1)}, u32[]{:S(2)}, u32[]{:S(2)}) collective-permute-start(bf16[4,16,192]{2,1,0:T(8,128)(2,1)S(1)} %slice.49), channel_id=1, source_target_pairs={{0,24},{8,0},{16,8},{24,16},{1,25},{9,1},{17,9},{25,17},{2,26},{10... | collective-permute-start | bytes 73736 | tf_op jit(solution)/shard_map/ppermute | solution.py:575
  13.7 3.0 %collective-permute-start.3 = (bf16[16,4,192]{2,1,0:T(4,128)(2,1)S(1)}, bf16[16,4,192]{2,1,0:T(4,128)(2,1)S(1)}, u32[]{:S(2)}, u32[]{:S(2)}) collective-permute-start(bf16[16,4,192]{2,1,0:T(4,128)(2,1)S(1)} %pad_maximum_fusion.6), channel_id=1, source_target_pairs={{0,7},{1,0},{2,1},{3,2},{4,3},{5,4},{6,5},{7,6},{8,15},{9,8},{10,9... | collective-permute-start | bytes 73736 | tf_op jit(solution)/shard_map/ppermute | solution.py:575
  15.6 2.3 %collective-permute-start.1 = (bf16[16,4,192]{2,1,0:T(4,128)(2,1)S(1)}, bf16[16,4,192]{2,1,0:T(4,128)(2,1)S(1)}, u32[]{:S(2)}, u32[]{:S(2)}) collective-permute-start(bf16[16,4,192]{2,1,0:T(4,128)(2,1)S(1)} %pad_maximum_fusion.7), channel_id=1, source_target_pairs={{0,7},{1,0},{2,1},{3,2},{4,3},{5,4},{6,5},{7,6},{8,15},{9,8},{10,9... | collective-permute-start | bytes 73736 | tf_op jit(solution)/shard_map/ppermute | solution.py:575
  27.4 6.0 %collective-permute-start.6 = (bf16[4,16,192]{2,1,0:T(8,128)(2,1)S(1)}, bf16[4,16,192]{2,1,0:T(8,128)(2,1)S(1)}, u32[]{:S(2)}, u32[]{:S(2)}) collective-permute-start(bf16[4,16,192]{2,1,0:T(8,128)(2,1)S(1)} %slice.60), channel_id=1, source_target_pairs={{0,8},{8,16},{16,24},{24,0},{1,9},{9,17},{17,25},{25,1},{2,10},{10... | collective-permute-start | bytes 73736 | tf_op jit(solution)/shard_map/ppermute | solution.py:575
  31.5 5.7 %collective-permute-start.4 = (bf16[4,16,192]{2,1,0:T(8,128)(2,1)S(1)}, bf16[4,16,192]{2,1,0:T(8,128)(2,1)S(1)}, u32[]{:S(2)}, u32[]{:S(2)}) collective-permute-start(bf16[4,16,192]{2,1,0:T(8,128)(2,1)S(1)} %slice.56), channel_id=1, source_target_pairs={{0,8},{8,16},{16,24},{24,0},{1,9},{9,17},{17,25},{25,1},{2,10},{10... | collective-permute-start | bytes 73736 | tf_op jit(solution)/shard_map/ppermute | solution.py:575
  33.4 4.3 %collective-permute-start.7 = (bf16[16,4,192]{2,1,0:T(4,128)(2,1)S(1)}, bf16[16,4,192]{2,1,0:T(4,128)(2,1)S(1)}, u32[]{:S(2)}, u32[]{:S(2)}) collective-permute-start(bf16[16,4,192]{2,1,0:T(4,128)(2,1)S(1)} %pad_maximum_fusion.4), channel_id=1, source_target_pairs={{0,1},{1,2},{2,3},{3,4},{4,5},{5,6},{6,7},{7,0},{8,9},{9,10},{10,1... | collective-permute-start | bytes 73736 | tf_op jit(solution)/shard_map/ppermute | solution.py:575
  37.2 54.9 %collective-permute-start.5 = (bf16[16,4,192]{2,1,0:T(4,128)(2,1)S(1)}, bf16[16,4,192]{2,1,0:T(4,128)(2,1)S(1)}, u32[]{:S(2)}, u32[]{:S(2)}) collective-permute-start(bf16[16,4,192]{2,1,0:T(4,128)(2,1)S(1)} %pad_maximum_fusion.5), channel_id=1, source_target_pairs={{0,1},{1,2},{2,3},{3,4},{4,5},{5,6},{6,7},{7,0},{8,9},{9,10},{10,1... | collective-permute-start | bytes 73736 | tf_op jit(solution)/shard_map/ppermute | solution.py:575

commit v2 on v1

--- a/solution.py
+++ b/solution.py
@@ -49,6 +49,39 @@
             piece = values[at : at + WIN * WIN].reshape(WIN, WIN, values.shape[-1])
             ref[r : r + WIN, c : c + WIN, :] = piece.astype(ref.dtype)
             at += WIN * WIN
+
+
+def edges(shape, direction):
+    half = WIN // 2
+    leave, land = [], []
+    for size in shape[:2]:
+        first, rest = slice(0, half), slice(half, size)
+        body, last = slice(0, size - half), slice(size - half, size)
+        leave.append((rest, first) if direction < 0 else (body, last))
+        land.append((body, last) if direction < 0 else (rest, first))
+    order = ((0, 0), (1, 0), (0, 1), (1, 1))
+    return (
+        [(leave[0][a], leave[1][b]) for a, b in order],
+        [(land[0][a], land[1][b]) for a, b in order],
+    )
+
+
+def strip_shapes(shape):
+    half = WIN // 2
+    height, breadth, channels = shape
+    return [(half, breadth - half, channels), (height - half, half, channels), (half, half, channels)]
+
+
+def store_strips(refs, tile, direction):
+    for ref, at in zip(refs, edges(tile.shape, direction)[0][1:]):
+        ref[...] = tile[at].astype(ref.dtype)
+
+
+def join_tile(scratch, tile_ref, strip_refs, direction):
+    leave, land = edges(tile_ref.shape, direction)
+    scratch[land[0]] = tile_ref[...].astype(F32)[leave[0]]
+    for ref, at in zip(strip_refs, land[1:]):
+        scratch[at] = ref[...].astype(F32)
 
 
 def norm_parts(x):
@@ -306,12 +339,16 @@
 
     def body(x_ref, *refs):
         w = weight_view(refs[: len(KEYS)], 0)
-        out_ref, packed_ref, mixed_ref, mid_ref, pre_ref, pos_ref = refs[len(KEYS) :]
+        out_ref, packed_ref, mixed_ref, mid_ref, pre_ref, pos_ref = refs[len(KEYS) : len(KEYS) + 6]
+        strip_refs, tile = refs[len(KEYS) + 6 : len(KEYS) + 9], refs[-1]
         x = load_windows(x_ref, height, breadth)
         position = position_stack(w["rel"], heads)
         pos_ref[...] = position
         out, saved = forward(x, w, position, None, heads)
-        store_windows(out_ref, out.astype(F32), height, breadth)
+        store_windows(tile, out.astype(F32), height, breadth)
+        moved = tile[...]
+        out_ref[...] = moved.astype(BF16)
+        store_strips(strip_refs, moved, -1)
         for ref, value in zip((packed_ref, mixed_ref, mid_ref, pre_ref), saved):
             ref[...] = value
 
@@ -322,7 +359,7 @@
         shape_of((tokens, channels), BF16),
         shape_of((tokens, mlp), F32),
         shape_of((heads * WIN * WIN, WIN * WIN), F32),
-    ]
+    ] + [shape_of(strip, BF16) for strip in strip_shapes(imagery.shape)]
     return pl.pallas_call(
         body,
         name="fwd0",
@@ -330,53 +367,68 @@
         out_shape=outs,
         in_specs=[whole(imagery.shape)] + weight_specs(params, 0),
         out_specs=[whole(o.shape) for o in outs],
+        scratch_shapes=[pltpu.VMEM(imagery.shape, F32)],
     )(imagery, *params)
 
 
-def second_both(moved, grad, start, params, total_rows, total_cols, grad_rows):
+def second_both(moved, moved_strips, grad, grad_strips, start, params, total_rows, total_cols, grad_rows):
     height, breadth, channels = moved.shape
     heads = params[4].shape[0]
     width = params[9].shape[2]
 
     def body(start_ref, x_ref, g_ref, *refs):
+        tile, light_ref = refs[-2:]
+        join_tile(tile, x_ref, refs[:3], -1)
+        x = load_windows(tile, height, breadth)
+        join_tile(tile, g_ref, refs[3:6], -1)
+        g = load_windows(tile, height, breadth)
+        refs = refs[6:]
         w = weight_view(refs[: len(KEYS)], 1)
-        out_ref, dx_ref, grads_ref, light_ref = refs[len(KEYS) :]
-        x = load_windows(x_ref, height, breadth)
+        out_ref, dx_ref, grads_ref = refs[len(KEYS) : len(KEYS) + 3]
+        out_strips, dx_strips = refs[len(KEYS) + 3 : len(KEYS) + 6], refs[len(KEYS) + 6 : len(KEYS) + 9]
         position = position_stack(w["rel"], heads)
         masks = zone_masks(start_ref, height, breadth, total_rows, total_cols, heads)
         out, saved = forward(x, w, position, masks, heads)
-        store_windows(out_ref, out.astype(F32), height, breadth)
-        g = load_windows(g_ref, height, breadth)
         dx = backward(x, g, saved, w, position, masks, heads, grads_ref, light_ref)
-        store_windows(dx_ref, dx, height, breadth)
+        for ref, strips, value in (
+            (out_ref, out_strips, out.astype(F32)),
+            (dx_ref, dx_strips, dx),
+        ):
+            store_windows(tile, value, height, breadth)
+            whole_tile = tile[...]
+            ref[...] = whole_tile.astype(BF16)
+            store_strips(strips, whole_tile, 1)
 
     outs = [
         shape_of(moved.shape, BF16),
         shape_of(moved.shape, BF16),
         shape_of((grad_rows, width), BF16),
-    ]
+    ] + [shape_of(strip, BF16) for strip in strip_shapes(moved.shape) * 2]
     return pl.pallas_call(
         body,
         name="both1",
         grid=(1,),
         out_shape=outs,
         in_specs=[pl.BlockSpec(memory_space=pltpu.SMEM), whole(moved.shape), whole(moved.shape)]
+        + [whole(strip.shape) for strip in (*moved_strips, *grad_strips)]
         + weight_specs(params, 1),
         out_specs=[whole(o.shape) for o in outs],
-        scratch_shapes=[pltpu.VMEM((16, width), F32)],
-    )(start, moved, grad, *params)
-
-
-def first_backward(imagery, grad, saved, params, grad_rows):
+        scratch_shapes=[pltpu.VMEM(moved.shape, F32), pltpu.VMEM((16, width), F32)],
+    )(start, moved, grad, *moved_strips, *grad_strips, *params)
+
+
+def first_backward(imagery, grad, grad_strips, saved, params, grad_rows):
     height, breadth, channels = imagery.shape
     heads = params[4].shape[0]
     width = params[9].shape[2]
 
     def body(x_ref, g_ref, packed_ref, mixed_ref, mid_ref, pre_ref, pos_ref, *refs):
         w = weight_view(refs[: len(KEYS)], 0)
-        dx_ref, grads_ref, light_ref = refs[len(KEYS) :]
+        strip_refs = refs[len(KEYS) : len(KEYS) + 3]
+        dx_ref, grads_ref, tile, light_ref = refs[len(KEYS) + 3 :]
         x = load_windows(x_ref, height, breadth)
-        g = load_windows(g_ref, height, breadth)
+        join_tile(tile, g_ref, strip_refs, 1)
+        g = load_windows(tile, height, breadth)
         values = (packed_ref[...], mixed_ref[...], mid_ref[...], pre_ref[...])
         dx = backward(x, g, values, w, pos_ref[...], None, heads, grads_ref, light_ref)
         store_windows(dx_ref, dx, height, breadth)
@@ -389,10 +441,11 @@
         out_shape=outs,
         in_specs=[whole(imagery.shape), whole(grad.shape)]
         + [whole(s.shape) for s in saved]
-        + weight_specs(params, 0),
+        + weight_specs(params, 0)
+        + [whole(strip.shape) for strip in grad_strips],
         out_specs=[whole(o.shape) for o in outs],
-        scratch_shapes=[pltpu.VMEM((16, width), F32)],
-    )(imagery, grad, *saved, *params)
+        scratch_shapes=[pltpu.VMEM(imagery.shape, F32), pltpu.VMEM((16, width), F32)],
+    )(imagery, grad, *saved, *params, *grad_strips)
 
 
 def sum_all(grads_one, grads_two, nz, nq):
@@ -569,31 +622,20 @@
     )(summed)
 
 
-def from_behind(value, axis, steps):
-    count = lax.axis_size(axis)
-    pairs = [(source, (source + steps) % count) for source in range(count)]
-    return lax.ppermute(value, axis, pairs)
-
-
-def along_axis(values, axis, name, direction):
-    half = WIN // 2
-    size = values.shape[axis]
-    if direction < 0:
-        outgoing = lax.slice_in_dim(values, 0, half, axis=axis)
-        kept = lax.slice_in_dim(values, half, size, axis=axis)
-    else:
-        outgoing = lax.slice_in_dim(values, size - half, size, axis=axis)
-        kept = lax.slice_in_dim(values, 0, size - half, axis=axis)
-    arrived = from_behind(outgoing, name, direction)
-    return jnp.concatenate([kept, arrived] if direction < 0 else [arrived, kept], axis=axis)
-
-
-def advance(values):
-    return along_axis(along_axis(values, 0, "rows", -1), 1, "cols", -1)
-
-
-def retreat(values):
-    return along_axis(along_axis(values, 0, "rows", 1), 1, "cols", 1)
+def travel(strips, direction):
+    nz, nc = lax.axis_size("rows"), lax.axis_size("cols")
+    rows = [(i, (i + direction) % nz) for i in range(nz)]
+    cols = [(i, (i + direction) % nc) for i in range(nc)]
+    both = [
+        (r * nc + c, (r + direction) % nz * nc + (c + direction) % nc)
+        for r in range(nz)
+        for c in range(nc)
+    ]
+    return [
+        lax.ppermute(strips[0], "rows", rows),
+        lax.ppermute(strips[1], "cols", cols),
+        lax.ppermute(strips[2], ("rows", "cols"), both),
+    ]
 
 
 def per_device(imagery, cotangent, *params):
@@ -610,12 +652,31 @@
     ).astype(jnp.int32)
     unit = nz * (nc // 2) * 8
     grad_rows = -(-(3 * channels + 16) // unit) * unit
-    level_one, *saved = first_forward(imagery, params)
-    level_two, back_two, grads_two = second_both(
-        advance(level_one), advance(cotangent), start, params, total_rows, total_cols, grad_rows
+    grad_strips = travel([cotangent[at] for at in edges(cotangent.shape, -1)[0][1:]], -1)
+    level_one, *rest = first_forward(imagery, params)
+    saved, strips = rest[:5], rest[5:]
+    level_two, back_two, grads_two, *strips = second_both(
+        level_one,
+        travel(strips, -1),
+        cotangent,
+        grad_strips,
+        start,
+        params,
+        total_rows,
+        total_cols,
+        grad_rows,
     )
-    output = retreat(level_two)
-    back_one, grads_one = first_backward(imagery, retreat(back_two), saved, params, grad_rows)
+    back_strips = travel(strips[3:], 1)
+    back_one, grads_one = first_backward(imagery, back_two, back_strips, saved, params, grad_rows)
+    half = WIN // 2
+    row_strip, col_strip, corner = travel(strips[:3], 1)
+    output = jnp.concatenate(
+        [
+            jnp.concatenate([corner, row_strip], axis=1),
+            jnp.concatenate([col_strip, level_two[:-half, :-half]], axis=1),
+        ],
+        axis=0,
+    )
     summed = sum_all(grads_one, grads_two, nz, nc // 2)
     merged = unpack(summed, params, float(total_rows * total_cols) ** (-0.5))
     merged = list(merged)

time: 93.4 us -> 98.8 us (1.058)
  starting transfers between devices: 9.57 us -> 13.5 us
  waiting for transfers between devices: 7.13 us -> 9.95 us
  Pallas kernels: 66 us -> 68.3 us
  other arithmetic: 3.57 us -> 1.3 us
  local copies, waits for them, and re-layouts: 5.82 us -> 4.4 us
    ppermute x8 -> x12, starting transfers between devices: 9.57 us -> 13.5 us  [the longest x4 6.46 us: travel(): lax.ppermute(strips[2], ('rows', 'cols'), both)]
    ppermute x8 -> x12, waiting for transfers between devices: 7.13 us -> 9.95 us  [the longest x4 8.42 us: travel(): lax.ppermute(strips[2], ('rows', 'cols'), both)]
    slice x8 -> x4, local copies, waits for them, and re-layouts: 5.82 us -> 3.2 us  [the longest x3 2.3 us: per_device(): cotangent[at]]
    concatenate x8 -> x1, other arithmetic: 2.94 us -> 0.71 us  [per_device(): jnp.concatenate([jnp.concatenate([corner, row_strip], axis=1), jnp.concat...]
    pallas_call x1, Pallas kernels: 42.8 us -> 44.9 us  [sum_all(): pl.pallas_call(body, name='sum_all', out_shape=shape_of((rows, width), BF...]
    unnamed x2 -> x18, local copies, waits for them, and re-layouts: 0.01 us -> 1.2 us
  transfers between devices with their start and end apart: 8 -> 12, of which waited for: 6 -> 3; matrix products, arithmetic and copies ran while one was open for 7% -> 3% of each run, Pallas kernels for 63% -> 61%
where the time goes in v2:
time: 98.8 us; the launch traced here: 98.3 us
  Pallas kernels  68.3 us (69%)
  starting transfers between devices  13.5 us (14%)
  waiting for transfers between devices  9.95 us (10%)
  local copies, waits for them, and re-layouts  4.4 us (4%)
  other arithmetic  1.3 us (1%)
    pallas_call x1, Pallas kernels, sum_all(): pl.pallas_call(body, name='sum_all', out_shape=shape_of((rows, width), BF...  44.9 us
    ppermute x4, waiting for transfers between devices, travel(): lax.ppermute(strips[2], ('rows', 'cols'), both)  8.42 us
    pallas_call x1, Pallas kernels, second_both(): pl.pallas_call(body, name='both1', grid=(1,), out_shape=outs, in_specs=[p...  8.05 us
    pallas_call x1, Pallas kernels, first_backward(): pl.pallas_call(body, name='bwd0', grid=(1,), out_shape=outs, in_specs=[wh...  7.33 us
    ppermute x4, starting transfers between devices, travel(): lax.ppermute(strips[2], ('rows', 'cols'), both)  6.46 us
    pallas_call x1, Pallas kernels, first_forward(): pl.pallas_call(body, name='fwd0', grid=(1,), out_shape=outs, in_specs=[wh...  4.41 us
    ppermute x4, starting transfers between devices, travel(): lax.ppermute(strips[0], 'rows', rows)  4.16 us
    pallas_call x1, Pallas kernels, unpack(): pl.pallas_call(body, name='unpack', grid=(1,), out_shape=outs, in_specs=[...  3.62 us
  transfers between devices with their start and end apart: 12, of which 3 were waited for; matrix products, arithmetic and copies ran while one was open for 3% of the time, Pallas kernels for 61%

profile of v2, /device:TPU:0, one launch (start us, length us, event | category | flops | bytes accessed | tf_op | source)
XLA Modules:
  0.0 98.3 jit_solution(12504432420755014166)
XLA Ops:
  0.6 0.7 slice.14
  1.4 6.4 %collective-permute-start.5 = (bf16[4,4,192]{2,1,0:T(4,128)(2,1)S(1)}, bf16[4,4,192]{2,1,0:T(4,128)(2,1)S(1)}, u32[]{:S(2)}, u32[]{:S(2)}) collective-permute-start(bf16[4,4,192]{2,1,0:T(4,128)(2,1)S(1)} %slice.14), channel_id=1, source_target_pairs={{0,31},{1,24},{2,25},{3,26},{4,27},{5,28},{6,29},{7,30},{8,7},{9,0... | collective-permute-start | bytes 18440 | tf_op jit(solution)/shard_map/ppermute | solution.py:637
  7.8 0.8 slice.13
  8.6 0.9 collective-permute-start.4
  9.5 0.8 slice.12
  10.2 0.5 collective-permute-start.3
  10.8 4.4 %fwd0.1 = (bf16[16,16,192]{2,1,0:T(8,128)(2,1)}, bf16[256,576]{1,0:T(8,128)(2,1)}, bf16[256,192]{1,0:T(8,128)(2,1)}, bf16[256,192]{1,0:T(8,128)(2,1)}, f32[256,7...) custom-call(bf16[16,16,192]{2,1,0:T(8,128)(2,1)} %x_ref.3, ...), custom_call_target="tpu_custom_call" | custom-call | tf_op jit(solution)/shard_map/fwd0/pallas_call | solution.py:363
  15.2 0.1 collective-permute-start.2
  15.2 0.7 collective-permute-start.1
  15.9 0.5 collective-permute-start
  16.4 0.6 pad_add_fusion.start_ref
  17.0 1.5 %collective-permute-done.2.refs_2_ = bf16[4,4,192]{2,1,0:T(4,128)(2,1)S(1)} collective-permute-done((bf16[4,4,192]{2,1,0:T(4,128)(2,1)}, bf16[4,4,192]{2,1,0:T(4,128)(2,1)S(1)}, u32[]{:S(2)}, u32[]{:S(2)}) %collective-permute-start.2) | collective-permute-done | bytes 6176 | tf_op jit(solution)/shard_map/ppermute | solution.py:637
  18.5 1.5 %collective-permute-done.refs_0_ = bf16[4,12,192]{2,1,0:T(8,128)(2,1)S(1)} collective-permute-done((bf16[4,12,192]{2,1,0:T(8,128)(2,1)}, bf16[4,12,192]{2,1,0:T(8,128)(2,1)S(1)}, u32[]{:S(2)}, u32[]{:S(2)}) %collective-permute-start) | collective-permute-done | bytes 18464 | tf_op jit(solution)/shard_map/ppermute | solution.py:635
  20.1 0.6 copy-done.2
  20.7 8.1 %both1.1 = (bf16[16,16,192]{2,1,0:T(8,128)(2,1)}, bf16[16,16,192]{2,1,0:T(8,128)(2,1)}, bf16[640,768]{1,0:T(8,128)(2,1)}, bf16[4,12,192]{2,1,0:T(8,128)(2,1)}, b...) custom-call(s32[2]{0:T(128)} %pad_add_fusion.start_ref, ...), custom_call_target="tpu_custom_call" | custom-call | tf_op jit(solution)/shard_map/both1/pallas_call | solution.py:407
  28.7 0.1 collective-permute-start.10
  28.8 1.6 %collective-permute-start.9 = (bf16[4,12,192]{2,1,0:T(8,128)(2,1)}, bf16[4,12,192]{2,1,0:T(8,128)(2,1)S(1)}, u32[]{:S(2)}, u32[]{:S(2)}) collective-permute-start(bf16[4,12,192]{2,1,0:T(8,128)(2,1)} %get-tuple-element.62), channel_id=1, source_target_pairs={{0,8},{8,16},{16,24},{24,0},{1,9},{9,17},{17,25},{25,1},{2,10},{10... | collective-permute-start | bytes 55304 | tf_op jit(solution)/shard_map/ppermute | solution.py:635
  30.4 1.3 %collective-permute-start.8 = (bf16[12,4,192]{2,1,0:T(4,128)(2,1)}, bf16[12,4,192]{2,1,0:T(4,128)(2,1)S(1)}, u32[]{:S(2)}, u32[]{:S(2)}) collective-permute-start(bf16[12,4,192]{2,1,0:T(4,128)(2,1)} %get-tuple-element.54), channel_id=1, source_target_pairs={{0,1},{1,2},{2,3},{3,4},{4,5},{5,6},{6,7},{7,0},{8,9},{9,10},{10,1... | collective-permute-start | bytes 55304 | tf_op jit(solution)/shard_map/ppermute | solution.py:636
  31.7 1.6 %collective-permute-start.7 = (bf16[4,12,192]{2,1,0:T(8,128)(2,1)}, bf16[4,12,192]{2,1,0:T(8,128)(2,1)S(1)}, u32[]{:S(2)}, u32[]{:S(2)}) collective-permute-start(bf16[4,12,192]{2,1,0:T(8,128)(2,1)} %get-tuple-element.53), channel_id=1, source_target_pairs={{0,8},{8,16},{16,24},{24,0},{1,9},{9,17},{17,25},{25,1},{2,10},{10... | collective-permute-start | bytes 55304 | tf_op jit(solution)/shard_map/ppermute | solution.py:635
  33.3 0.0 collective-permute-start.11
  33.3 6.9 %collective-permute-done.11.refs_15_ = bf16[4,4,192]{2,1,0:T(4,128)(2,1)S(1)} collective-permute-done((bf16[4,4,192]{2,1,0:T(4,128)(2,1)}, bf16[4,4,192]{2,1,0:T(4,128)(2,1)S(1)}, u32[]{:S(2)}, u32[]{:S(2)}) %collective-permute-start.11) | collective-permute-done | bytes 6176 | tf_op jit(solution)/shard_map/ppermute | solution.py:637
  40.1 0.0 collective-permute-start.6
  40.1 0.9 slice.15
  41.1 0.0 collective-permute-done.9.refs_13_
  41.1 0.6 copy-done.5
  41.7 0.0 copy-done.1
  41.7 7.3 %bwd0.1 = (bf16[16,16,192]{2,1,0:T(8,128)(2,1)}, bf16[640,768]{1,0:T(8,128)(2,1)}) custom-call(bf16[16,16,192]{2,1,0:T(8,128)(2,1)} %x_ref.3, bf16[16,16,192]{2,1,0:T(8,128)(2,1)} %get-tuple-element.56.g_ref, bf16[256,576]{1,0:T(8,128)(2,1)} %get-tuple-element.57.packed_ref, bf16[256,192]{1,0:T(8,128)(2,1)} %get-tuple-element.58.mixed_ref, ...), custom_call_target="tpu_custom_call" | custom-call | tf_op jit(solution)/shard_map/bwd0/pallas_call | solution.py:437
  49.0 44.9 %sum_all.1.s_ref = bf16[1280,768]{1,0:T(8,128)(2,1)} custom-call(bf16[640,768]{1,0:T(8,128)(2,1)} %get-tuple-element.66.one_ref, bf16[640,768]{1,0:T(8,128)(2,1)} %get-tuple-element.67.two_ref), custom_call_target="tpu_custom_call" | custom-call | tf_op jit(solution)/shard_map/sum_all/pallas_call | solution.py:567
  93.9 3.6 %unpack.1 = (f32[2,192]{1,0:T(2,128)}, f32[2,192]{1,0:T(2,128)}, f32[2,192,576]{2,1,0:T(8,128)}, f32[2,576]{1,0:T(2,128)}, f32[6,2,225]{2,1,0:T(2,128)}, /*index...) custom-call(bf16[1280,768]{1,0:T(8,128)(2,1)} %sum_all.1.s_ref), custom_call_target="tpu_custom_call" | custom-call | tf_op jit(solution)/shard_map/unpack/pallas_call | solution.py:615
  97.6 0.0 collective-permute-done.8
  97.6 0.0 collective-permute-done.7
  97.6 0.7 maximum_maximum_fusion
  (21 shorter events, 0.0 us)
Async XLA Ops:
  1.4 14.6 %collective-permute-start.5 = (bf16[4,4,192]{2,1,0:T(4,128)(2,1)S(1)}, bf16[4,4,192]{2,1,0:T(4,128)(2,1)S(1)}, u32[]{:S(2)}, u32[]{:S(2)}) collective-permute-start(bf16[4,4,192]{2,1,0:T(4,128)(2,1)S(1)} %slice.14), channel_id=1, source_target_pairs={{0,31},{1,24},{2,25},{3,26},{4,27},{5,28},{6,29},{7,30},{8,7},{9,0... | collective-permute-start | bytes 18440 | tf_op jit(solution)/shard_map/ppermute | solution.py:637
  8.6 9.9 %collective-permute-start.4 = (bf16[12,4,192]{2,1,0:T(4,128)(2,1)S(1)}, bf16[12,4,192]{2,1,0:T(4,128)(2,1)S(1)}, u32[]{:S(2)}, u32[]{:S(2)}) collective-permute-start(bf16[12,4,192]{2,1,0:T(4,128)(2,1)S(1)} %slice.13), channel_id=1, source_target_pairs={{0,7},{1,0},{2,1},{3,2},{4,3},{5,4},{6,5},{7,6},{8,15},{9,8},{10,9... | collective-permute-start | bytes 55304 | tf_op jit(solution)/shard_map/ppermute | solution.py:636
  10.2 8.3 %collective-permute-start.3 = (bf16[4,12,192]{2,1,0:T(8,128)(2,1)S(1)}, bf16[4,12,192]{2,1,0:T(8,128)(2,1)S(1)}, u32[]{:S(2)}, u32[]{:S(2)}) collective-permute-start(bf16[4,12,192]{2,1,0:T(8,128)(2,1)S(1)} %slice.12), channel_id=1, source_target_pairs={{0,24},{8,0},{16,8},{24,16},{1,25},{9,1},{17,9},{25,17},{2,26},{10... | collective-permute-start | bytes 55304 | tf_op jit(solution)/shard_map/ppermute | solution.py:635
  15.2 3.3 %collective-permute-start.2 = (bf16[4,4,192]{2,1,0:T(4,128)(2,1)}, bf16[4,4,192]{2,1,0:T(4,128)(2,1)S(1)}, u32[]{:S(2)}, u32[]{:S(2)}) collective-permute-start(bf16[4,4,192]{2,1,0:T(4,128)(2,1)} %get-tuple-element.51), channel_id=1, source_target_pairs={{0,31},{1,24},{2,25},{3,26},{4,27},{5,28},{6,29},{7,30},{8,7},{9,0... | collective-permute-start | bytes 18440 | tf_op jit(solution)/shard_map/ppermute | solution.py:637
  15.2 3.3 %collective-permute-start.1 = (bf16[12,4,192]{2,1,0:T(4,128)(2,1)}, bf16[12,4,192]{2,1,0:T(4,128)(2,1)S(1)}, u32[]{:S(2)}, u32[]{:S(2)}) collective-permute-start(bf16[12,4,192]{2,1,0:T(4,128)(2,1)} %get-tuple-element.50), channel_id=1, source_target_pairs={{0,7},{1,0},{2,1},{3,2},{4,3},{5,4},{6,5},{7,6},{8,15},{9,8},{10,9... | collective-permute-start | bytes 55304 | tf_op jit(solution)/shard_map/ppermute | solution.py:636
  15.9 4.1 %copy-start.6 = (bf16[4,4,192]{2,1,0:T(4,128)(2,1)}, bf16[4,4,192]{2,1,0:T(4,128)(2,1)S(1)}, u32[]{:S(2)}) copy-start(bf16[4,4,192]{2,1,0:T(4,128)(2,1)S(1)} %collective-permute-done.5.refs_5_) | copy-start | bytes 18436
  15.9 4.1 %collective-permute-start = (bf16[4,12,192]{2,1,0:T(8,128)(2,1)}, bf16[4,12,192]{2,1,0:T(8,128)(2,1)S(1)}, u32[]{:S(2)}, u32[]{:S(2)}) collective-permute-start(bf16[4,12,192]{2,1,0:T(8,128)(2,1)} %get-tuple-element.49), channel_id=1, source_target_pairs={{0,24},{8,0},{16,8},{24,16},{1,25},{9,1},{17,9},{25,17},{2,26},{10... | collective-permute-start | bytes 55304 | tf_op jit(solution)/shard_map/ppermute | solution.py:635
  18.5 1.6 %copy-start.7 = (bf16[4,4,192]{2,1,0:T(4,128)(2,1)}, bf16[4,4,192]{2,1,0:T(4,128)(2,1)S(1)}, u32[]{:S(2)}) copy-start(bf16[4,4,192]{2,1,0:T(4,128)(2,1)S(1)} %collective-permute-done.2.refs_2_) | copy-start | bytes 18436
  18.5 1.6 %copy-start.3 = (bf16[12,4,192]{2,1,0:T(4,128)(2,1)}, bf16[12,4,192]{2,1,0:T(4,128)(2,1)S(1)}, u32[]{:S(2)}) copy-start(bf16[12,4,192]{2,1,0:T(4,128)(2,1)S(1)} %collective-permute-done.4.refs_4_) | copy-start | bytes 55300
  18.5 1.6 %copy-start = (bf16[4,12,192]{2,1,0:T(8,128)(2,1)}, bf16[4,12,192]{2,1,0:T(8,128)(2,1)S(1)}, u32[]{:S(2)}) copy-start(bf16[4,12,192]{2,1,0:T(8,128)(2,1)S(1)} %collective-permute-done.3.refs_3_) | copy-start | bytes 55300
  18.5 1.5 %copy-start.4 = (bf16[12,4,192]{2,1,0:T(4,128)(2,1)}, bf16[12,4,192]{2,1,0:T(4,128)(2,1)S(1)}, u32[]{:S(2)}) copy-start(bf16[12,4,192]{2,1,0:T(4,128)(2,1)S(1)} %collective-permute-done.1.refs_1_) | copy-start | bytes 55300
  20.1 0.6 copy-start.2
  28.7 12.3 %collective-permute-start.10 = (bf16[12,4,192]{2,1,0:T(4,128)(2,1)}, bf16[12,4,192]{2,1,0:T(4,128)(2,1)S(1)}, u32[]{:S(2)}, u32[]{:S(2)}) collective-permute-start(bf16[12,4,192]{2,1,0:T(4,128)(2,1)} %get-tuple-element.63), channel_id=1, source_target_pairs={{0,1},{1,2},{2,3},{3,4},{4,5},{5,6},{6,7},{7,0},{8,9},{9,10},{10,1... | collective-permute-start | bytes 55304 | tf_op jit(solution)/shard_map/ppermute | solution.py:636
  28.8 12.3 %collective-permute-start.9 = (bf16[4,12,192]{2,1,0:T(8,128)(2,1)}, bf16[4,12,192]{2,1,0:T(8,128)(2,1)S(1)}, u32[]{:S(2)}, u32[]{:S(2)}) collective-permute-start(bf16[4,12,192]{2,1,0:T(8,128)(2,1)} %get-tuple-element.62), channel_id=1, source_target_pairs={{0,8},{8,16},{16,24},{24,0},{1,9},{9,17},{17,25},{25,1},{2,10},{10... | collective-permute-start | bytes 55304 | tf_op jit(solution)/shard_map/ppermute | solution.py:635
  30.4 67.2 %collective-permute-start.8 = (bf16[12,4,192]{2,1,0:T(4,128)(2,1)}, bf16[12,4,192]{2,1,0:T(4,128)(2,1)S(1)}, u32[]{:S(2)}, u32[]{:S(2)}) collective-permute-start(bf16[12,4,192]{2,1,0:T(4,128)(2,1)} %get-tuple-element.54), channel_id=1, source_target_pairs={{0,1},{1,2},{2,3},{3,4},{4,5},{5,6},{6,7},{7,0},{8,9},{9,10},{10,1... | collective-permute-start | bytes 55304 | tf_op jit(solution)/shard_map/ppermute | solution.py:636
  31.7 65.9 %collective-permute-start.7 = (bf16[4,12,192]{2,1,0:T(8,128)(2,1)}, bf16[4,12,192]{2,1,0:T(8,128)(2,1)S(1)}, u32[]{:S(2)}, u32[]{:S(2)}) collective-permute-start(bf16[4,12,192]{2,1,0:T(8,128)(2,1)} %get-tuple-element.53), channel_id=1, source_target_pairs={{0,8},{8,16},{16,24},{24,0},{1,9},{9,17},{17,25},{25,1},{2,10},{10... | collective-permute-start | bytes 55304 | tf_op jit(solution)/shard_map/ppermute | solution.py:635
  33.3 6.9 %collective-permute-start.11 = (bf16[4,4,192]{2,1,0:T(4,128)(2,1)}, bf16[4,4,192]{2,1,0:T(4,128)(2,1)S(1)}, u32[]{:S(2)}, u32[]{:S(2)}) collective-permute-start(bf16[4,4,192]{2,1,0:T(4,128)(2,1)} %get-tuple-element.64), channel_id=1, source_target_pairs={{0,9},{1,10},{2,11},{3,12},{4,13},{5,14},{6,15},{7,8},{8,17},{9,18... | collective-permute-start | bytes 18440 | tf_op jit(solution)/shard_map/ppermute | solution.py:637
  40.1 0.9 copy-start.8
  40.1 57.4 %collective-permute-start.6 = (bf16[4,4,192]{2,1,0:T(4,128)(2,1)}, bf16[4,4,192]{2,1,0:T(4,128)(2,1)S(1)}, u32[]{:S(2)}, u32[]{:S(2)}) collective-permute-start(bf16[4,4,192]{2,1,0:T(4,128)(2,1)} %get-tuple-element.52), channel_id=1, source_target_pairs={{0,9},{1,10},{2,11},{3,12},{4,13},{5,14},{6,15},{7,8},{8,17},{9,18... | collective-permute-start | bytes 18440 | tf_op jit(solution)/shard_map/ppermute | solution.py:637
  41.0 0.6 copy-start.5
  41.1 0.6 copy-start.1
